TPU v7x, 32 devices: a whole 2x2x4 slice. The times are simulated.
32 devices in a mesh: ctx: 8 (over z, x), head: 4 (over y, core).
Axes of the slice: x: 2, y: 2, z: 4, core: 2. Of those that a mesh axis runs over, the one named last changes fastest.
Arguments:
- signal: bfloat16 [6144, 5120], P(('ctx', 'head')), may hold values from -0.125 to 0.125
- cotangent: bfloat16 [6144, 5120], P(('ctx', 'head')), may hold values from -0.125 to 0.125
- input_map: bfloat16 [6144, 128], P('ctx'), may hold values from -1.75 to 1.75
- output_map: bfloat16 [6144, 128], P('ctx'), may hold values from -1.75 to 1.75
- log_decay: float32 [6144, 80], P('ctx', 'head'), may hold values from -1 to 0, as said below
- skip_gain: float32 [80], P('head'), may hold values from 0.5 to 2
Outputs:
- scan_out: bfloat16 [6144, 5120], P(('ctx', 'head'))
- grad_signal: bfloat16 [6144, 5120], P(('ctx', 'head'))
- grad_input_map: float32 [6144, 128], P('ctx')
- grad_output_map: float32 [6144, 128], P('ctx')
- grad_decay: float32 [6144, 80], P('ctx', 'head')
Inputs may be any that keep to these rules, and one draw needn't show every extreme that they name: `log_decay`: every entry is negative.
All inputs are finite; a program needn't handle non-finite values.
Results may differ from a plain program's by a relative error of at most 0.0027.
Values may be sent and summed in bfloat16 or wider, within the bound.
A program may use at most 192 MiB of HBM per device.

v0:
```python
import jax
import jax.numpy as jnp
from jax import lax
from jax.experimental import pallas as pl
from jax.experimental.pallas import tpu as pltpu
from jax.sharding import PartitionSpec as P

F32, BF16, F16 = jnp.float32, jnp.bfloat16, jnp.float16
TINY = 1e-30
STEP_HEADS = 8


def split(value):
    high = value.astype(BF16)
    return high, (value - high.astype(F32)).astype(BF16)


def dot(a, b, ca, cb):
    return lax.dot_general(a, b, (((ca,), (cb,)), ((), ())), preferred_element_type=F32)


def column(table, lanes, head):
    return jnp.sum(jnp.where(lanes == head, table, 0.0), axis=1, keepdims=True)


def states_kernel(x_ref, dy_ref, cum_ref, b_ref, c_ref, s_ref, r_ref, *, per, width):
    step = pl.program_id(0)
    cum = cum_ref[...]
    length = cum.shape[0]
    lanes = lax.broadcasted_iota(jnp.int32, cum.shape, 1)
    half = lax.broadcasted_iota(jnp.int32, (length, 2 * width), 1) < width
    into, outof = b_ref[...], c_ref[...]
    for pair in range(per // 2):
        first = column(cum, lanes, step * per + 2 * pair)
        second = column(cum, lanes, step * per + 2 * pair + 1)
        both = jnp.where(half, first, second)
        total = both[length - 1 : length, :]
        at = slice(pair * 2 * width, (pair + 1) * 2 * width)
        xs = split(x_ref[:, at].astype(F32) * jnp.exp(total - both))
        ds = split(dy_ref[:, at].astype(F32) * jnp.exp(both))
        s_ref[at, :] = dot(xs[0], into, 0, 0) + dot(xs[1], into, 0, 0)
        r_ref[at, :] = dot(ds[0], outof, 0, 0) + dot(ds[1], outof, 0, 0)


def within_kernel(
    x_ref, dy_ref, cum_ref, cumt_ref, b_ref, c_ref, gain_ref,
    y_ref, dx_ref, dsc_ref, rows_ref, cols_ref, scores_ref, *, per, width,
):
    step = pl.program_id(0)

    @pl.when(step == 0)
    def _():
        scores_ref[...] = dot(c_ref[...], b_ref[...], 1, 1)
        dsc_ref[...] = jnp.zeros_like(dsc_ref)
        rows_ref[...] = jnp.zeros_like(rows_ref)

    cum = cum_ref[...]
    length = cum.shape[0]
    lanes = lax.broadcasted_iota(jnp.int32, cum.shape, 1)
    causal = lax.broadcasted_iota(jnp.int32, (length, length), 0) >= lax.broadcasted_iota(
        jnp.int32, (length, length), 1
    )
    for pair in range(per // 2):
        outs, grads = [], []
        for h in (2 * pair, 2 * pair + 1):
            head = step * per + h
            at = slice(h * width, (h + 1) * width)
            x, dy = x_ref[:, at], dy_ref[:, at]
            col = column(cum, lanes, head)
            row = cumt_ref[h : h + 1, :]
            decay = jnp.exp(jnp.where(causal, col - row, -1e30))
            weights = scores_ref[...] * decay
            narrow = weights.astype(BF16)
            outs.append(dot(narrow, x, 1, 0))
            grads.append(dot(narrow, dy, 0, 0))
            dw = dot(dy, x, 1, 1).astype(BF16).astype(F32)
            dsc_ref[...] += dw * decay
            pull = dw * weights
            rows_ref[...] += jnp.where(lanes == head, jnp.sum(pull, axis=1, keepdims=True), 0.0)
            cols_ref[h : h + 1, :] = jnp.sum(pull, axis=0, keepdims=True)
        at = slice(pair * 2 * width, (pair + 1) * 2 * width)
        gain = gain_ref[:, at]
        y_ref[:, at] = jnp.concatenate(outs, axis=1) + gain * x_ref[:, at].astype(F32)
        dx_ref[:, at] = jnp.concatenate(grads, axis=1) + gain * dy_ref[:, at].astype(F32)


def carried_kernel(
    x_ref, dy_ref, y_ref, dx_ref, e_ref, l_ref, cum_ref, b_ref, c_ref, dsc_ref, net_ref,
    out_ref, grad_ref, db_ref, dc_ref, dla_ref, q_ref, r_ref, el_ref, *, per, width,
):
    step = pl.program_id(0)

    @pl.when(step == 0)
    def _():
        q_ref[...] = net_ref[...]
        r_ref[...] = jnp.zeros_like(r_ref)
        el_ref[...] = jnp.zeros_like(el_ref)
        high, low = split(dsc_ref[...])
        db_ref[...] = dot(high, c_ref[...], 0, 0) + dot(low, c_ref[...], 0, 0)
        dc_ref[...] = dot(high, b_ref[...], 1, 0) + dot(low, b_ref[...], 1, 0)

    cum = cum_ref[...]
    length = cum.shape[0]
    lanes = lax.broadcasted_iota(jnp.int32, cum.shape, 1)
    lane_row = lanes[0:1, :]
    half = lax.broadcasted_iota(jnp.int32, (length, 2 * width), 1) < width
    into, outof = b_ref[...], c_ref[...]
    add_b, add_c = jnp.zeros_like(db_ref), jnp.zeros_like(dc_ref)
    add_q, add_r, add_el = jnp.zeros_like(q_ref), jnp.zeros_like(r_ref), jnp.zeros_like(el_ref)
    for pair in range(per // 2):
        head = step * per + 2 * pair
        both = jnp.where(half, column(cum, lanes, head), column(cum, lanes, head + 1))
        total = both[length - 1 : length, :]
        grow, tail = jnp.exp(both), jnp.exp(total - both)
        at = slice(pair * 2 * width, (pair + 1) * 2 * width)
        x, dy = x_ref[:, at].astype(F32), dy_ref[:, at].astype(F32)
        entering, leaving = e_ref[at, :], l_ref[at, :]
        eh, el = split(entering)
        lh, ll = split(leaving)
        carried = (dot(outof, eh, 1, 1) + dot(outof, el, 1, 1)) * grow
        pulled = (dot(into, lh, 1, 1) + dot(into, ll, 1, 1)) * tail
        out_ref[:, at] = (y_ref[:, at] + carried).astype(BF16)
        grad_ref[:, at] = (dx_ref[:, at] + pulled).astype(BF16)
        zh, zl = split(dy * grow)
        add_c += dot(zh, eh, 1, 0) + dot(zl, eh, 1, 0) + dot(zh, el, 1, 0)
        uh, ul = split(x * tail)
        add_b += dot(uh, lh, 1, 0) + dot(ul, lh, 1, 0) + dot(uh, ll, 1, 0)
        q, r, prod = dy * carried, x * pulled, entering * leaving
        for h in (0, 1):
            mine = half if h == 0 else jnp.logical_not(half)
            mark = lanes == head + h
            add_q += jnp.where(mark, jnp.sum(jnp.where(mine, q, 0.0), axis=1, keepdims=True), 0.0)
            add_r += jnp.where(mark, jnp.sum(jnp.where(mine, r, 0.0), axis=1, keepdims=True), 0.0)
            part = jnp.sum(prod[h * width : (h + 1) * width, :], axis=0, keepdims=True)
            add_el += jnp.where(lane_row == head + h, jnp.sum(part, axis=1, keepdims=True), 0.0)
    db_ref[...] += add_b
    dc_ref[...] += add_c
    q_ref[...] += add_q
    r_ref[...] += add_r
    el_ref[...] += add_el

    @pl.when(step == pl.num_programs(0) - 1)
    def _():
        i = lax.broadcasted_iota(jnp.int32, (length, length), 0)
        j = lax.broadcasted_iota(jnp.int32, (length, length), 1)
        after, before = (j >= i).astype(BF16), (j < i).astype(BF16)
        qh, ql = split(q_ref[...])
        rh, rl = split(r_ref[...])
        dla_ref[...] = (
            dot(after, qh, 1, 0) + dot(after, ql, 1, 0) + dot(before, rh, 1, 0) + dot(before, rl, 1, 0)
            + jnp.exp(cum[length - 1 : length, :]) * el_ref[...]
        )


def later_sum(logs, own=None):
    count = logs.shape[0]
    i = lax.broadcasted_iota(jnp.int32, (count, count), 0)
    j = lax.broadcasted_iota(jnp.int32, (count, count), 1)
    keep = (j > i) if own is None else (j > i) & (j < own)
    return jnp.sum(jnp.where(keep[:, :, None], logs[None], 0.0), axis=1)


def group_factors(meta, ctx, blocks, members):
    total, peak = meta[:, :, 0], meta[:, :, 1]
    to_end = jax.vmap(later_sum)(total)
    bound = jnp.sum(jnp.exp(to_end) * peak, axis=1)
    sums = jnp.sum(total, axis=1)
    earlier = lax.broadcasted_iota(jnp.int32, (blocks, 1), 0) < ctx
    reach = jnp.where(earlier, jnp.exp(later_sum(sums, ctx)), 0.0) * bound
    own_total = lax.dynamic_index_in_dim(total, ctx, 0, keepdims=False)
    own_peak = lax.dynamic_index_in_dim(peak, ctx, 0, keepdims=False)
    own_to_end = lax.dynamic_index_in_dim(to_end, ctx, 0, keepdims=False)
    limit = [jnp.sum(reach, axis=0)]
    for s in range(members - 1):
        limit.append(jnp.exp(own_total[s]) * limit[-1] + own_peak[s])
    return dict(
        peak=own_peak, factor=jnp.exp(own_to_end), keep=jnp.exp(own_total),
        bound=lax.dynamic_index_in_dim(bound, ctx, 0, keepdims=False),
        reach=reach, limit=jnp.stack(limit),
    )


def shards(signal, cotangent, input_map, output_map, log_decay, skip_gain):
    members, blocks = lax.axis_size("head"), lax.axis_size("ctx")
    member, ctx = lax.axis_index("head"), lax.axis_index("ctx")
    length, channels = signal.shape
    own_heads = log_decay.shape[1]
    heads = own_heads * members
    width = channels // heads
    state = input_map.shape[1]
    per = STEP_HEADS
    steps = heads // per
    lane_block = per * width

    decay = lax.all_to_all(log_decay, "head", split_axis=0, concat_axis=1, tiled=True)
    gains = lax.all_gather(skip_gain, "head", tiled=True)
    into = lax.dynamic_slice_in_dim(input_map, member * length, length, 0)
    outof = lax.dynamic_slice_in_dim(output_map, member * length, length, 0)
    lower = (
        lax.broadcasted_iota(jnp.int32, (length, length), 0)
        >= lax.broadcasted_iota(jnp.int32, (length, length), 1)
    ).astype(F32)
    cum = jnp.dot(lower, decay, precision=lax.Precision.HIGHEST)
    cum_t = cum.T
    gain_row = jnp.repeat(gains, width)[None, :]

    wide = pl.BlockSpec((length, lane_block), lambda k: (0, k))
    tall = pl.BlockSpec((lane_block, state), lambda k: (k, 0))

    def whole(*shape):
        return pl.BlockSpec(shape, lambda k: (0, 0))

    def call(body, name, in_specs, out_specs, out_shape, scratch=(), flops=0):
        return pl.pallas_call(
            lambda *refs: body(*refs, per=per, width=width),
            grid=(steps,), in_specs=in_specs, out_specs=out_specs, out_shape=out_shape,
            scratch_shapes=scratch, name=name,
            cost_estimate=pl.CostEstimate(flops=flops, transcendentals=0, bytes_accessed=16 * length * channels),
        )

    sd = jax.ShapeDtypeStruct
    maps = [whole(length, state)] * 2
    own_state, own_seed = call(
        states_kernel, "states", [wide, wide, whole(length, heads)] + maps, [tall, tall],
        [sd((channels, state), F32)] * 2, flops=8 * length * channels * state,
    )(signal, cotangent, cum, into, outof)

    def peak_of(value):
        return jnp.maximum(jnp.max(jnp.abs(value.reshape(heads, -1)), axis=1), TINY)

    own_meta = jnp.stack([cum[-1], peak_of(own_state), peak_of(own_seed)])
    meta = lax.all_gather(own_meta, ("ctx", "head")).reshape(blocks, members, 3, heads)

    def scaled(value, scale):
        return value.reshape(heads, width, state) / scale[:, None, None]

    packed = jnp.concatenate(
        [scaled(own_state, own_meta[1]), scaled(own_seed, own_meta[2])], axis=2
    ).astype(F16)
    arrived = lax.all_to_all(packed, "head", split_axis=0, concat_axis=0, tiled=True)
    arrived = arrived.reshape(members, own_heads, width, 2 * state).astype(F32)

    y_local, dx_local, dscores, rows, cols = call(
        within_kernel, "within",
        [wide, wide, whole(length, heads), pl.BlockSpec((per, length), lambda k: (k, 0))] + maps
        + [pl.BlockSpec((1, lane_block), lambda k: (0, k))],
        [wide, wide, whole(length, length), whole(length, heads),
         pl.BlockSpec((per, length), lambda k: (k, 0))],
        [sd((length, channels), F32)] * 2
        + [sd((length, length), F32), sd((length, heads), F32), sd((heads, length), F32)],
        scratch=[pltpu.VMEM((length, length), F32)], flops=24 * length * length * channels,
    )(signal, cotangent, cum, cum_t, into, outof, gain_row)

    forward = group_factors(meta[:, :, (0, 1)], ctx, blocks, members)
    back = group_factors(meta[::-1, ::-1, (0, 2)], blocks - 1 - ctx, blocks, members)

    def mine(table):
        return lax.dynamic_slice_in_dim(table, member * own_heads, own_heads, table.ndim - 1)[
            ..., None, None
        ]

    fwd = {k: mine(v) for k, v in forward.items()}
    bwd = {k: mine(v) for k, v in back.items()}
    parts_f = arrived[..., :state] * fwd["peak"]
    parts_b = arrived[::-1, ..., state:] * bwd["peak"]
    group_f = jnp.sum(parts_f * fwd["factor"], axis=0) / jnp.maximum(fwd["bound"], TINY)
    group_b = jnp.sum(parts_b * bwd["factor"], axis=0) / jnp.maximum(bwd["bound"], TINY)
    sums = lax.all_gather(jnp.concatenate([group_f, group_b], axis=2).astype(F16), "ctx").astype(F32)
    entering = jnp.sum(sums[..., :state] * fwd["reach"], axis=0)
    leaving = jnp.sum(sums[..., state:] * bwd["reach"][::-1], axis=0)
    list_f, list_b = [entering], [leaving]
    for s in range(members - 1):
        list_f.append(fwd["keep"][s] * list_f[-1] + parts_f[s])
        list_b.append(bwd["keep"][s] * list_b[-1] + parts_b[s])
    send_f = jnp.stack(list_f) / jnp.maximum(fwd["limit"], TINY)
    send_b = (jnp.stack(list_b) / jnp.maximum(bwd["limit"], TINY))[::-1]
    send = jnp.concatenate([send_f, send_b], axis=3).astype(F16)
    back_home = lax.all_to_all(
        send.reshape(heads, width, 2 * state), "head", split_axis=0, concat_axis=0, tiled=True
    ).astype(F32)
    limit_f = lax.dynamic_index_in_dim(forward["limit"], member, 0, keepdims=False)
    limit_b = lax.dynamic_index_in_dim(back["limit"], members - 1 - member, 0, keepdims=False)
    e_all = (back_home[..., :state] * limit_f[:, None, None]).reshape(channels, state)
    l_all = (back_home[..., state:] * limit_b[:, None, None]).reshape(channels, state)

    scan_out, grad_signal, grad_in, grad_out, grad_decay = call(
        carried_kernel, "carried",
        [wide, wide, wide, wide, tall, tall, whole(length, heads)] + maps
        + [whole(length, length), whole(length, heads)],
        [wide, wide, whole(length, state), whole(length, state), whole(length, heads)],
        [sd((length, channels), BF16)] * 2 + [sd((length, state), F32)] * 2 + [sd((length, heads), F32)],
        scratch=[pltpu.VMEM((length, heads), F32)] * 2 + [pltpu.VMEM((1, heads), F32)],
        flops=20 * length * channels * state,
    )(signal, cotangent, y_local, dx_local, e_all, l_all, cum, into, outof, dscores, rows - cols.T)

    maps_out = lax.all_gather(jnp.concatenate([grad_in, grad_out], axis=1), "head", tiled=True)
    grad_decay = lax.all_to_all(grad_decay, "head", split_axis=1, concat_axis=0, tiled=True)
    return (scan_out, grad_signal, maps_out[:, :state], maps_out[:, state:], grad_decay)


def solution(mesh):
    return jax.shard_map(
        shards,
        mesh=mesh,
        in_specs=(
            P(("ctx", "head"), None),
            P(("ctx", "head"), None),
            P("ctx", None),
            P("ctx", None),
            P("ctx", "head"),
            P("head"),
        ),
        out_specs=(
            P(("ctx", "head"), None),
            P(("ctx", "head"), None),
            P("ctx", None),
            P("ctx", None),
            P("ctx", "head"),
        ),
        check_vma=False,
    )
```

profile of v0, /device:TPU:0, one launch (start us, length us, event | category | flops | bytes accessed | tf_op | source)
XLA Modules:
  0.0 323.7 jit_solution(3411587535597618670)
XLA Ops:
  0.6 1.0 all_to_all.34
  2.3 4.3 %all-to-all-start = ((f32[4,192,20]{1,2,0:T(8,128)}), f32[4,192,20]{1,2,0:T(8,128)S(1)}, u32[]{:S(2)}, u32[]{:S(2)}) async-start(f32[4,192,20]{1,2,0:T(8,128)} %copy.66), calls=%async_computation | async-start | bytes 196608 | tf_op jit(solution)/shard_map/all_to_all | solution.py:195
  6.9 1.5 constant_dynamic-slice_fusion.24
  8.5 2.3 all-to-all-done
  12.0 11.8 %states.1 = (f32[5120,128]{1,0:T(8,128)}, f32[5120,128]{1,0:T(8,128)}) custom-call(bf16[192,5120]{1,0:T(8,128)(2,1)} %refs_0_.5, bf16[192,5120]{1,0:T(8,128)(2,1)} %refs_1_.5, f32[192,80]{1,0:T(8,128)} %copy.67.refs_2_.refs_6_, bf16[192,128]{1,0:T(8,128)(2,1)} %get-tuple-element.75.refs_4_.refs_3_.refs_7_, ...), custom_call_target="tpu_custom_call" | custom-call | flops 1006632960 | bytes 15728640 | tf_op jit(solution)/shard_map/states/pallas_call | solution.py:223
  23.8 2.6 abs_reduce_fusion.1
  27.6 41.3 %all-gather.1 = f32[32,3,80]{2,1,0:T(4,128)S(1)} all-gather(f32[1,3,80]{2,1,0:T(4,128)S(1)} %maximum_bitcast_fusion), channel_id=2, replica_groups=mesh['ctx'=8,'head'=4] {'ctx','head'}, dimensions={0}, use_global_device_ids=true | all-gather | bytes 31680 | tf_op jit(solution)/shard_map/all_gather | solution.py:232
  69.9 2.2 divide_convert_fusion.1
  72.6 2.6 pad_maximum_fusion
  75.1 3.7 %all-to-all-start.1 = ((f16[80,64,256]{2,1,0:T(8,128)(2,1)}), f16[80,64,256]{2,1,0:T(8,128)(2,1)S(1)}, u32[]{:S(2)}, u32[]{:S(2)}) async-start(f16[80,64,256]{2,1,0:T(8,128)(2,1)} %pad_maximum_fusion), calls=%async_computation.1 | async-start | bytes 5242880 | tf_op jit(solution)/shard_map/all_to_all | solution.py:240
  81.0 29.0 %all-to-all-done.1 = f16[80,64,256]{2,1,0:T(8,128)(2,1)S(1)} async-done(((f16[80,64,256]{2,1,0:T(8,128)(2,1)}), f16[80,64,256]{2,1,0:T(8,128)(2,1)S(1)}, u32[]{:S(2)}, u32[]{:S(2)}) %all-to-all-start.1) | async-done | bytes 2621472 | tf_op jit(solution)/shard_map/all_to_all | solution.py:240
  112.2 101.3 %all-gather.3 = f16[8,20,64,256]{3,2,1,0:T(8,128)(2,1)S(1)} all-gather(f16[1,20,64,256]{3,2,1,0:T(8,128)(2,1)S(1)} %pad_maximum_fusion.3), channel_id=1, replica_groups=mesh['ctx'=8,'head'=4] {'ctx'}, dimensions={0}, use_global_device_ids=true | all-gather | bytes 5898240 | tf_op jit(solution)/shard_map/all_gather | solution.py:268
  213.5 1.3 convert_element_type.26
  214.8 1.1 fusion.1
  217.7 2.6 pad_maximum_fusion.2
  220.3 3.8 %all-to-all-start.2 = ((f16[80,64,256]{2,1,0:T(8,128)(2,1)}), f16[80,64,256]{2,1,0:T(8,128)(2,1)S(1)}, u32[]{:S(2)}, u32[]{:S(2)}) async-start(f16[80,64,256]{2,1,0:T(8,128)(2,1)} %pad_maximum_fusion.2), calls=%async_computation.2 | async-start | bytes 5242880 | tf_op jit(solution)/shard_map/all_to_all | solution.py:278
  225.6 31.2 %all-reduce = f32[80]{0:T(128)S(1)} all-reduce(f32[80]{0:T(128)S(1)} %dynamic-update-slice), channel_id=1, replica_groups=mesh['ctx'=8,'head'=4] {'head'}, use_global_device_ids=true, to_apply=%add | all-reduce | flops 80 | bytes 640
  257.6 27.9 %within.1 = (f32[192,5120]{1,0:T(8,128)}, f32[192,5120]{1,0:T(8,128)}, f32[192,192]{1,0:T(8,128)}, f32[192,80]{1,0:T(8,128)}, f32[80,192]{1,0:T(8,128)}) custom-call(bf16[192,5120]{1,0:T(8,128)(2,1)} %refs_0_.5, bf16[192,5120]{1,0:T(8,128)(2,1)} %refs_1_.5, f32[192,80]{1,0:T(8,128)} %copy.67.refs_2_.refs_6_, f32[80,192]{1,0:T(8,128)} %bitcast.164, ...), custom_call_target="tpu_custom_call" | custom-call | flops 4529848320 | bytes 15728640 | tf_op jit(solution)/shard_map/within/pallas_call | solution.py:243
  285.5 1.0 copy.75
  286.5 1.5 bitcast_subtract_fusion.refs_10_
  288.7 2.8 slice_multiply_fusion.2
  291.4 15.6 %carried.1 = (bf16[192,5120]{1,0:T(8,128)(2,1)}, bf16[192,5120]{1,0:T(8,128)(2,1)}, f32[192,128]{1,0:T(8,128)}, f32[192,128]{1,0:T(8,128)}, f32[192,80]{1,0:T(8,128)}) custom-call(bf16[192,5120]{1,0:T(8,128)(2,1)} %refs_0_.5, bf16[192,5120]{1,0:T(8,128)(2,1)} %refs_1_.5, f32[192,5120]{1,0:T(8,128)} %get-tuple-element.17.refs_2_, ...), custom_call_target="tpu_custom_call" | custom-call | flops 2516582400 | bytes 15728640 | tf_op jit(solution)/shard_map/carried/pallas_call | solution.py:286
  308.6 3.3 %all-to-all-start.3 = ((f32[192,4,20]{0,2,1:T(8,128)}), f32[192,4,20]{0,2,1:T(8,128)S(1)}, u32[]{:S(2)}, u32[]{:S(2)}) async-start(f32[192,4,20]{0,2,1:T(8,128)} %all_to_all.40), calls=%async_computation.3 | async-start | bytes 196608 | tf_op jit(solution)/shard_map/all_to_all | solution.py:297
  312.9 9.1 %all_gather.20 = f32[768,256]{1,0:T(8,128)S(1)} all-gather(f32[192,256]{1,0:T(8,128)S(1)} %pad_maximum_fusion.4), channel_id=1, replica_groups=mesh['ctx'=8,'head'=4] {'head'}, dimensions={0}, use_global_device_ids=true | all-gather | bytes 983040 | tf_op jit(solution)/shard_map/all_gather | solution.py:296
  (106 shorter events, 17.3 us)
Async XLA Ops:
  2.3 8.6 %all-to-all-start = ((f32[4,192,20]{1,2,0:T(8,128)}), f32[4,192,20]{1,2,0:T(8,128)S(1)}, u32[]{:S(2)}, u32[]{:S(2)}) async-start(f32[4,192,20]{1,2,0:T(8,128)} %copy.66), calls=%async_computation | async-start | bytes 196608 | tf_op jit(solution)/shard_map/all_to_all | solution.py:195
  11.1 15.3 %copy-start.1 = (f32[192,80]{0,1:T(8,128)}, f32[192,80]{0,1:T(8,128)S(1)}, u32[]{:S(2)}) copy-start(f32[192,80]{0,1:T(8,128)S(1)} %fusion.5) | copy-start | bytes 184324
  23.8 2.9 copy-start
  75.1 34.9 %all-to-all-start.1 = ((f16[80,64,256]{2,1,0:T(8,128)(2,1)}), f16[80,64,256]{2,1,0:T(8,128)(2,1)S(1)}, u32[]{:S(2)}, u32[]{:S(2)}) async-start(f16[80,64,256]{2,1,0:T(8,128)(2,1)} %pad_maximum_fusion), calls=%async_computation.1 | async-start | bytes 5242880 | tf_op jit(solution)/shard_map/all_to_all | solution.py:240
  220.3 3.8 %copy-start.3 = (u32[32]{0:T(128)S(1)}, u32[32]{0:T(128)}, u32[]{:S(2)}) copy-start(u32[32]{0:T(128)} %constant.168) | copy-start | bytes 388
  220.3 5.1 %copy-start.2 = (f32[20]{0:T(128)S(1)}, f32[20]{0:T(128)}, u32[]{:S(2)}) copy-start(f32[20]{0:T(128)} %param.13) | copy-start | bytes 244
  220.3 67.8 %all-to-all-start.2 = ((f16[80,64,256]{2,1,0:T(8,128)(2,1)}), f16[80,64,256]{2,1,0:T(8,128)(2,1)S(1)}, u32[]{:S(2)}, u32[]{:S(2)}) async-start(f16[80,64,256]{2,1,0:T(8,128)(2,1)} %pad_maximum_fusion.2), calls=%async_computation.2 | async-start | bytes 5242880 | tf_op jit(solution)/shard_map/all_to_all | solution.py:278
  308.6 14.3 %all-to-all-start.3 = ((f32[192,4,20]{0,2,1:T(8,128)}), f32[192,4,20]{0,2,1:T(8,128)S(1)}, u32[]{:S(2)}, u32[]{:S(2)}) async-start(f32[192,4,20]{0,2,1:T(8,128)} %all_to_all.40), calls=%async_computation.3 | async-start | bytes 196608 | tf_op jit(solution)/shard_map/all_to_all | solution.py:297
where the time goes:
time: 325 us; the launch traced here: 324 us
  blocking collectives  183 us (56%)
  Pallas kernels  55.3 us (17%)
  waiting for transfers between devices  31.4 us (10%)
  other arithmetic  24.5 us (8%)
  starting transfers between devices  15 us (5%)
  local copies, waits for them, and re-layouts  12.6 us (4%)
    all_gather x1, blocking collectives, shards(): lax.all_gather(jnp.concatenate([group_f, group_b], axis=2).astype(F16), '...  101 us
    all_gather x1, blocking collectives, shards(): lax.all_gather(own_meta, ('ctx', 'head')).reshape(blocks, members, 3, heads)  41.3 us
    unnamed x1, blocking collectives  31.2 us
    all_to_all x1, waiting for transfers between devices, shards(): lax.all_to_all(packed, 'head', split_axis=0, concat_axis=0, tiled=True)  29 us
    pallas_call x1, Pallas kernels, shards(): call(within_kernel, 'within', [wide, wide, whole(length, heads), pl.Block...  27.9 us
    pallas_call x1, Pallas kernels, shards(): call(carried_kernel, 'carried', [wide, wide, wide, wide, tall, tall, whol...  15.6 us
    pallas_call x1, Pallas kernels, shards(): call(states_kernel, 'states', [wide, wide, whole(length, heads)] + maps,...  11.8 us
    all_gather x1, blocking collectives, shards(): lax.all_gather(jnp.concatenate([grad_in, grad_out], axis=1), 'head', tile...  9.09 us
  transfers between devices with their start and end apart: 4, of which 2 were waited for; matrix products, arithmetic and copies ran while one was open for 3% of the time, Pallas kernels for 9%

commit v1 on v0

--- a/solution.py
+++ b/solution.py
@@ -8,6 +8,7 @@
 F32, BF16, F16 = jnp.float32, jnp.bfloat16, jnp.float16
 TINY = 1e-30
 STEP_HEADS = 8
+TAIL_ROWS = 16
 
 
 def split(value):
@@ -152,37 +153,64 @@
         )
 
 
-def later_sum(logs, own=None):
-    count = logs.shape[0]
-    i = lax.broadcasted_iota(jnp.int32, (count, count), 0)
-    j = lax.broadcasted_iota(jnp.int32, (count, count), 1)
-    keep = (j > i) if own is None else (j > i) & (j < own)
-    return jnp.sum(jnp.where(keep[:, :, None], logs[None], 0.0), axis=1)
-
-
-def group_factors(meta, ctx, blocks, members):
-    total, peak = meta[:, :, 0], meta[:, :, 1]
-    to_end = jax.vmap(later_sum)(total)
-    bound = jnp.sum(jnp.exp(to_end) * peak, axis=1)
-    sums = jnp.sum(total, axis=1)
-    earlier = lax.broadcasted_iota(jnp.int32, (blocks, 1), 0) < ctx
-    reach = jnp.where(earlier, jnp.exp(later_sum(sums, ctx)), 0.0) * bound
-    own_total = lax.dynamic_index_in_dim(total, ctx, 0, keepdims=False)
-    own_peak = lax.dynamic_index_in_dim(peak, ctx, 0, keepdims=False)
-    own_to_end = lax.dynamic_index_in_dim(to_end, ctx, 0, keepdims=False)
-    limit = [jnp.sum(reach, axis=0)]
-    for s in range(members - 1):
-        limit.append(jnp.exp(own_total[s]) * limit[-1] + own_peak[s])
-    return dict(
-        peak=own_peak, factor=jnp.exp(own_to_end), keep=jnp.exp(own_total),
-        bound=lax.dynamic_index_in_dim(bound, ctx, 0, keepdims=False),
-        reach=reach, limit=jnp.stack(limit),
-    )
+def exponents(value):
+    peak = jnp.max(jnp.abs(value), axis=(-2, -1))
+    return jnp.ceil(jnp.log2(jnp.maximum(peak, TINY)))
+
+
+def lane_row(table, lanes):
+    pad = [(0, 0)] * (table.ndim - 1) + [(0, lanes - table.shape[-1])]
+    return jnp.pad(table, pad)[..., None, :]
+
+
+def pack(value, extra=()):
+    power = exponents(value)
+    lanes = value.shape[-1]
+    rows = (value * jnp.exp2(-power)[..., None, None]).astype(F16)
+    rows = rows.reshape(*value.shape[:-3], -1, lanes)
+    tail = jnp.concatenate([lane_row(t, lanes) for t in (power, *extra)], axis=-2).astype(F16)
+    pad = [(0, 0)] * (tail.ndim - 2) + [(0, TAIL_ROWS - tail.shape[-2]), (0, 0)]
+    return jnp.concatenate([rows, jnp.pad(tail, pad)], axis=-2)
+
+
+def unpack(rows, heads):
+    body, tail = rows[..., :-TAIL_ROWS, :], rows[..., -TAIL_ROWS:, :].astype(F32)
+    body = body.reshape(*body.shape[:-2], heads, -1, body.shape[-1]).astype(F32)
+    tail = tail[..., :heads]
+    return body * jnp.exp2(tail[..., 0, :])[..., None, None], tail
+
+
+def three(value):
+    terms = []
+    for _ in range(3):
+        terms.append(lax.reduce_precision(value, 5, 10))
+        value = value - terms[-1]
+    return terms
+
+
+def chain(total, log_total, axis, backward):
+    count = lax.axis_size(axis)
+    heads = total.shape[0]
+    own, own_log = total, log_total
+    entering, entering_log = jnp.zeros_like(total), jnp.zeros_like(log_total)
+    reach = 1
+    while reach < count:
+        pairs = [(i, i + reach) for i in range(count - reach)]
+        if backward:
+            pairs = [(b, a) for a, b in pairs]
+        sent = pack(own, three(own_log))
+        got, tail = unpack(lax.ppermute(sent, axis, pairs), heads)
+        got_log = tail[1] + tail[2] + tail[3]
+        entering = entering + jnp.exp(entering_log)[:, None, None] * got
+        own = own + jnp.exp(own_log)[:, None, None] * got
+        entering_log, own_log = entering_log + got_log, own_log + got_log
+        reach *= 2
+    return entering
 
 
 def shards(signal, cotangent, input_map, output_map, log_decay, skip_gain):
-    members, blocks = lax.axis_size("head"), lax.axis_size("ctx")
-    member, ctx = lax.axis_index("head"), lax.axis_index("ctx")
+    members = lax.axis_size("head")
+    member = lax.axis_index("head")
     length, channels = signal.shape
     own_heads = log_decay.shape[1]
     heads = own_heads * members
@@ -192,8 +220,13 @@
     steps = heads // per
     lane_block = per * width
 
-    decay = lax.all_to_all(log_decay, "head", split_axis=0, concat_axis=1, tiled=True)
-    gains = lax.all_gather(skip_gain, "head", tiled=True)
+    by_member = log_decay.reshape(members, length, own_heads)
+    gain_rows = jnp.broadcast_to(skip_gain, (members, 8, own_heads))
+    rates = lax.all_to_all(
+        jnp.concatenate([by_member, gain_rows], axis=1), "head", split_axis=0, concat_axis=0, tiled=True
+    )
+    rates = jnp.swapaxes(rates, 0, 1).reshape(length + 8, heads)
+    decay, gains = rates[:length], rates[length]
     into = lax.dynamic_slice_in_dim(input_map, member * length, length, 0)
     outof = lax.dynamic_slice_in_dim(output_map, member * length, length, 0)
     lower = (
@@ -225,20 +258,13 @@
         [sd((channels, state), F32)] * 2, flops=8 * length * channels * state,
     )(signal, cotangent, cum, into, outof)
 
-    def peak_of(value):
-        return jnp.maximum(jnp.max(jnp.abs(value.reshape(heads, -1)), axis=1), TINY)
-
-    own_meta = jnp.stack([cum[-1], peak_of(own_state), peak_of(own_seed)])
-    meta = lax.all_gather(own_meta, ("ctx", "head")).reshape(blocks, members, 3, heads)
-
-    def scaled(value, scale):
-        return value.reshape(heads, width, state) / scale[:, None, None]
-
-    packed = jnp.concatenate(
-        [scaled(own_state, own_meta[1]), scaled(own_seed, own_meta[2])], axis=2
-    ).astype(F16)
-    arrived = lax.all_to_all(packed, "head", split_axis=0, concat_axis=0, tiled=True)
-    arrived = arrived.reshape(members, own_heads, width, 2 * state).astype(F32)
+    def swap(f, b):
+        both = jnp.concatenate([pack(f), pack(b)], axis=-1)
+        both = lax.all_to_all(both, "head", split_axis=0, concat_axis=0, tiled=True)
+        return [unpack(half, own_heads)[0] for half in (both[..., :state], both[..., state:])]
+
+    shape = (members, own_heads, width, state)
+    parts_f, parts_b = swap(own_state.reshape(shape), own_seed.reshape(shape))
 
     y_local, dx_local, dscores, rows, cols = call(
         within_kernel, "within",
@@ -251,37 +277,20 @@
         scratch=[pltpu.VMEM((length, length), F32)], flops=24 * length * length * channels,
     )(signal, cotangent, cum, cum_t, into, outof, gain_row)
 
-    forward = group_factors(meta[:, :, (0, 1)], ctx, blocks, members)
-    back = group_factors(meta[::-1, ::-1, (0, 2)], blocks - 1 - ctx, blocks, members)
-
-    def mine(table):
-        return lax.dynamic_slice_in_dim(table, member * own_heads, own_heads, table.ndim - 1)[
-            ..., None, None
-        ]
-
-    fwd = {k: mine(v) for k, v in forward.items()}
-    bwd = {k: mine(v) for k, v in back.items()}
-    parts_f = arrived[..., :state] * fwd["peak"]
-    parts_b = arrived[::-1, ..., state:] * bwd["peak"]
-    group_f = jnp.sum(parts_f * fwd["factor"], axis=0) / jnp.maximum(fwd["bound"], TINY)
-    group_b = jnp.sum(parts_b * bwd["factor"], axis=0) / jnp.maximum(bwd["bound"], TINY)
-    sums = lax.all_gather(jnp.concatenate([group_f, group_b], axis=2).astype(F16), "ctx").astype(F32)
-    entering = jnp.sum(sums[..., :state] * fwd["reach"], axis=0)
-    leaving = jnp.sum(sums[..., state:] * bwd["reach"][::-1], axis=0)
-    list_f, list_b = [entering], [leaving]
+    logs = jnp.sum(by_member, axis=1)
+    keep = jnp.exp(logs)[:, :, None, None]
+    group_f, group_b = parts_f[0], parts_b[-1]
+    for s in range(1, members):
+        group_f = keep[s] * group_f + parts_f[s]
+        group_b = keep[members - 1 - s] * group_b + parts_b[members - 1 - s]
+    group_log = jnp.sum(logs, axis=0)
+    list_f = [chain(group_f, group_log, "ctx", False)]
+    list_b = [chain(group_b, group_log, "ctx", True)]
     for s in range(members - 1):
-        list_f.append(fwd["keep"][s] * list_f[-1] + parts_f[s])
-        list_b.append(bwd["keep"][s] * list_b[-1] + parts_b[s])
-    send_f = jnp.stack(list_f) / jnp.maximum(fwd["limit"], TINY)
-    send_b = (jnp.stack(list_b) / jnp.maximum(bwd["limit"], TINY))[::-1]
-    send = jnp.concatenate([send_f, send_b], axis=3).astype(F16)
-    back_home = lax.all_to_all(
-        send.reshape(heads, width, 2 * state), "head", split_axis=0, concat_axis=0, tiled=True
-    ).astype(F32)
-    limit_f = lax.dynamic_index_in_dim(forward["limit"], member, 0, keepdims=False)
-    limit_b = lax.dynamic_index_in_dim(back["limit"], members - 1 - member, 0, keepdims=False)
-    e_all = (back_home[..., :state] * limit_f[:, None, None]).reshape(channels, state)
-    l_all = (back_home[..., state:] * limit_b[:, None, None]).reshape(channels, state)
+        list_f.append(keep[s] * list_f[-1] + parts_f[s])
+        list_b.append(keep[members - 1 - s] * list_b[-1] + parts_b[members - 1 - s])
+    e_all, l_all = swap(jnp.stack(list_f), jnp.stack(list_b[::-1]))
+    e_all, l_all = e_all.reshape(channels, state), l_all.reshape(channels, state)
 
     scan_out, grad_signal, grad_in, grad_out, grad_decay = call(
         carried_kernel, "carried",

time: 325 us -> 251 us (0.77)
  blocking collectives: 183 us -> 9.09 us
  other arithmetic: 24.5 us -> 57.5 us
  waiting for transfers between devices: 31.4 us -> 62.5 us
  starting transfers between devices: 15 us -> 34.2 us
  local copies, waits for them, and re-layouts: 12.6 us -> 28.5 us
    all_gather x2 -> x0, blocking collectives: 143 us -> none  [the longest x1 101 us: shards(): lax.all_gather(jnp.concatenate([group_f, group_b], axis=2).astype(F16), '...]
    unnamed x1 -> x0, blocking collectives: 31.2 us -> none
    ppermute x0 -> x6, waiting for transfers between devices: none -> 29.1 us  [chain(): got, tail = unpack(lax.ppermute(sent, axis, pairs), heads)]
    ppermute x0 -> x6, starting transfers between devices: none -> 19.2 us  [chain(): got, tail = unpack(lax.ppermute(sent, axis, pairs), heads)]
    convert_element_type x3 -> x17, other arithmetic: 2.47 us -> 21.1 us  [the longest x7 14.7 us: pack(): rows = (value * jnp.exp2(-power)[..., None, None]).astype(F16)]
    add x4, other arithmetic: 0.53 us -> 7.85 us  [the longest x2 4.09 us: chain(): entering = entering + jnp.exp(entering_log)[:, None, None] * got]
    reduce_max x4 -> x9, other arithmetic: 3.6 us -> 10.3 us  [exponents(): peak = jnp.max(jnp.abs(value), axis=(-2, -1))]
    broadcast_in_dim x1 -> x19, local copies, waits for them, and re-layouts: 0.01 us -> 5.69 us  [the longest x18 4.96 us: lane_row(): return jnp.pad(table, pad)[..., None, :]]
  transfers between devices with their start and end apart: 4 -> 10, of which waited for: 2 -> 8; matrix products, arithmetic and copies ran while one was open for 3% -> 5% of each run, Pallas kernels for 9% -> 11%
where the time goes in v1:
time: 251 us; the launch traced here: 249 us
  waiting for transfers between devices  62.5 us (25%)
  other arithmetic  57.5 us (23%)
  Pallas kernels  55.3 us (22%)
  starting transfers between devices  34.2 us (14%)
  local copies, waits for them, and re-layouts  28.5 us (11%)
  blocking collectives  9.09 us (4%)
    all_to_all x2, waiting for transfers between devices, swap(): both = lax.all_to_all(both, 'head', split_axis=0, concat_axis=0, tiled=True)  30.6 us
    ppermute x6, waiting for transfers between devices, chain(): got, tail = unpack(lax.ppermute(sent, axis, pairs), heads)  29.1 us
    pallas_call x1, Pallas kernels, shards(): call(within_kernel, 'within', [wide, wide, whole(length, heads), pl.Block...  27.9 us
    ppermute x6, starting transfers between devices, chain(): got, tail = unpack(lax.ppermute(sent, axis, pairs), heads)  19.2 us
    pallas_call x1, Pallas kernels, shards(): call(carried_kernel, 'carried', [wide, wide, wide, wide, tall, tall, whol...  15.5 us
    convert_element_type x7, other arithmetic, pack(): rows = (value * jnp.exp2(-power)[..., None, None]).astype(F16)  14.7 us
    pallas_call x1, Pallas kernels, shards(): call(states_kernel, 'states', [wide, wide, whole(length, heads)] + maps,...  11.8 us
    reduce_max x9, other arithmetic, exponents(): peak = jnp.max(jnp.abs(value), axis=(-2, -1))  10.3 us
  transfers between devices with their start and end apart: 10, of which 8 were waited for; matrix products, arithmetic and copies ran while one was open for 5% of the time, Pallas kernels for 11%

profile of v1, /device:TPU:0, one launch (start us, length us, event | category | flops | bytes accessed | tf_op | source)
XLA Modules:
  0.0 248.9 jit_solution(11250448749888906006)
XLA Ops:
  3.1 4.3 %all-to-all-start = ((f32[4,200,20]{1,2,0:T(8,128)}), f32[4,200,20]{1,2,0:T(8,128)S(1)}, u32[]{:S(2)}, u32[]{:S(2)}) async-start(f32[4,200,20]{1,2,0:T(8,128)} %copy.105), calls=%async_computation | async-start | bytes 196608 | tf_op jit(solution)/shard_map/all_to_all | solution.py:225
  8.9 2.8 %all-to-all-done = f32[4,200,20]{1,2,0:T(8,128)S(1)} async-done(((f32[4,200,20]{1,2,0:T(8,128)}), f32[4,200,20]{1,2,0:T(8,128)S(1)}, u32[]{:S(2)}, u32[]{:S(2)}) %all-to-all-start) | async-done | bytes 64032 | tf_op jit(solution)/shard_map/all_to_all | solution.py:225
  12.7 11.8 %states.1 = (f32[5120,128]{1,0:T(8,128)}, f32[5120,128]{1,0:T(8,128)}) custom-call(bf16[192,5120]{1,0:T(8,128)(2,1)} %refs_0_.5, bf16[192,5120]{1,0:T(8,128)(2,1)} %refs_1_.5, f32[192,80]{1,0:T(8,128)} %copy.106.refs_2_.refs_6_, bf16[192,128]{1,0:T(8,128)(2,1)} %get-tuple-element.132.refs_4_.refs_3_.refs_7_, ...), custom_call_target="tpu_custom_call" | custom-call | flops 1006632960 | bytes 15728640 | tf_op jit(solution)/shard_map/states/pallas_call | solution.py:256
  24.5 2.6 %abs_reduce_fusion.1 = f32[5120]{0:T(1024)S(1)} fusion(f32[5120,128]{1,0:T(8,128)} %get-tuple-element.19), kind=kLoop, calls=%fused_computation.34 | loop fusion | flops 1305600 | bytes 2641920 | tf_op jit(solution)/shard_map/reduce_max | solution.py:157
  33.7 3.8 %all-to-all-start.1 = ((f16[4,1296,256]{2,1,0:T(8,128)(2,1)}), f16[4,1296,256]{2,1,0:T(8,128)(2,1)S(1)}, u32[]{:S(2)}, u32[]{:S(2)}) async-start(f16[4,1296,256]{2,1,0:T(8,128)(2,1)} %fusion.11), calls=%async_computation.1 | async-start | bytes 5308416 | tf_op jit(solution)/shard_map/all_to_all | solution.py:263
  38.6 30.5 %all-to-all-done.1 = f16[4,1296,256]{2,1,0:T(8,128)(2,1)S(1)} async-done(((f16[4,1296,256]{2,1,0:T(8,128)(2,1)}), f16[4,1296,256]{2,1,0:T(8,128)(2,1)S(1)}, u32[]{:S(2)}, u32[]{:S(2)}) %all-to-all-start.1) | async-done | bytes 2654240 | tf_op jit(solution)/shard_map/all_to_all | solution.py:263
  75.3 3.8 %multiply_convert_fusion.7 = (f16[1280,128]{1,0:T(8,128)(2,1)S(1)}, f32[1280,128]{1,0:T(8,128)}, f16[1280,128]{1,0:T(8,128)(2,1)S(1)}, f32[1280,128]{1,0:T(8,128)}) fusion(f32[1280]{0:T(1024)S(1)} %mul.777, f32[1,20,64,128]{3,2,1,0:T(8,128)} %get-tuple-element.74, f32[1,20,64,128]{3,2,1,0:T(8,128)} %get-tuple-element.75, ...), kind=kLoop, calls=%fused_computation.86 | loop fusion | flops 2621440 | bytes 7239680 | tf_op jit(solution)/shard_map/convert_element_type | solution.py:169
  80.6 4.6 %collective-permute-start = (f16[1296,128]{1,0:T(8,128)(2,1)S(1)}, f16[1296,128]{1,0:T(8,128)(2,1)S(1)}, u32[]{:S(2)}, u32[]{:S(2)}) collective-permute-start(f16[1296,128]{1,0:T(8,128)(2,1)S(1)} %fusion.30), channel_id=1, source_target_pairs={{0,4},{4,8},{8,12},{12,16},{16,20},{20,24},{24,28},{1,5},{5,9},{9,... | collective-permute-start | bytes 995336 | tf_op jit(solution)/shard_map/ppermute | solution.py:202
  85.2 5.4 %collective-permute-done.3 = f16[1296,128]{1,0:T(8,128)(2,1)S(1)} collective-permute-done((f16[1296,128]{1,0:T(8,128)(2,1)S(1)}, f16[1296,128]{1,0:T(8,128)(2,1)S(1)}, u32[]{:S(2)}, u32[]{:S(2)}) %collective-permute-start.3) | collective-permute-done | bytes 331808 | tf_op jit(solution)/shard_map/ppermute | solution.py:202
  90.6 7.2 %collective-permute-done = f16[1296,128]{1,0:T(8,128)(2,1)S(1)} collective-permute-done((f16[1296,128]{1,0:T(8,128)(2,1)S(1)}, f16[1296,128]{1,0:T(8,128)(2,1)S(1)}, u32[]{:S(2)}, u32[]{:S(2)}) %collective-permute-start) | collective-permute-done | bytes 331808 | tf_op jit(solution)/shard_map/ppermute | solution.py:202
  106.1 2.3 multiply_convert_fusion.6
  110.0 4.6 %collective-permute-start.1 = (f16[1296,128]{1,0:T(8,128)(2,1)S(1)}, f16[1296,128]{1,0:T(8,128)(2,1)S(1)}, u32[]{:S(2)}, u32[]{:S(2)}) collective-permute-start(f16[1296,128]{1,0:T(8,128)(2,1)S(1)} %pad_maximum_fusion), channel_id=1, source_target_pairs={{0,8},{4,12},{8,16},{12,20},{16,24},{20,28},{1,9},{5,13},{9,17},{1... | collective-permute-start | bytes 995336 | tf_op jit(solution)/shard_map/ppermute | solution.py:202
  114.5 5.6 %collective-permute-done.4 = f16[1296,128]{1,0:T(8,128)(2,1)S(1)} collective-permute-done((f16[1296,128]{1,0:T(8,128)(2,1)S(1)}, f16[1296,128]{1,0:T(8,128)(2,1)S(1)}, u32[]{:S(2)}, u32[]{:S(2)}) %collective-permute-start.4) | collective-permute-done | bytes 331808 | tf_op jit(solution)/shard_map/ppermute | solution.py:202
  128.5 2.4 abs_reduce_fusion.5
  133.0 3.8 %multiply_convert_fusion.5 = (f16[1280,128]{1,0:T(8,128)(2,1)S(1)}, f16[1280,128]{1,0:T(8,128)(2,1)S(1)}) fusion(f32[1280]{0:T(1024)S(1)} %mul.816, f32[1280]{0:T(1024)S(1)} %mul.808, f32[1280]{0:T(1024)S(1)} %mul.800, f16[1296,128]{1,0:T(8,128)(2,1)} %copy-done.21, f32[1280,128]{1,0:T(8,128)} %get-tuple-element.58, f32[1280]{0:T(1024)S(1)} %mul.781, ...), kind=kLoop, calls=%fused_computation.80 | loop fusion | flops 3276800 | bytes 3322880 | tf_op jit(solution)/shard_map/convert_element_type | solution.py:169
  139.8 6.2 %collective-permute-start.2 = (f16[1296,128]{1,0:T(8,128)(2,1)}, f16[1296,128]{1,0:T(8,128)(2,1)}, u32[]{:S(2)}, u32[]{:S(2)}) collective-permute-start(f16[1296,128]{1,0:T(8,128)(2,1)} %pad_maximum_fusion.1), channel_id=1, source_target_pairs={{0,16},{4,20},{8,24},{12,28},{1,17},{5,21},{9,25},{13,29},{2,18},{... | collective-permute-start | bytes 995336 | tf_op jit(solution)/shard_map/ppermute | solution.py:202
  146.0 9.5 %collective-permute-done.5 = f16[1296,128]{1,0:T(8,128)(2,1)S(1)} collective-permute-done((f16[1296,128]{1,0:T(8,128)(2,1)S(1)}, f16[1296,128]{1,0:T(8,128)(2,1)S(1)}, u32[]{:S(2)}, u32[]{:S(2)}) %collective-permute-start.5) | collective-permute-done | bytes 331808 | tf_op jit(solution)/shard_map/ppermute | solution.py:202
  174.0 3.7 %all-to-all-start.2 = ((f16[4,1296,256]{2,1,0:T(8,128)(2,1)}), f16[4,1296,256]{2,1,0:T(8,128)(2,1)S(1)}, u32[]{:S(2)}, u32[]{:S(2)}) async-start(f16[4,1296,256]{2,1,0:T(8,128)(2,1)} %fusion.13), calls=%async_computation.2 | async-start | bytes 5308416 | tf_op jit(solution)/shard_map/all_to_all | solution.py:263
  178.7 27.9 %within.1 = (f32[192,5120]{1,0:T(8,128)}, f32[192,5120]{1,0:T(8,128)}, f32[192,192]{1,0:T(8,128)}, f32[192,80]{1,0:T(8,128)}, f32[80,192]{1,0:T(8,128)}) custom-call(bf16[192,5120]{1,0:T(8,128)(2,1)} %refs_0_.5, bf16[192,5120]{1,0:T(8,128)(2,1)} %refs_1_.5, f32[192,80]{1,0:T(8,128)} %copy.106.refs_2_.refs_6_, f32[80,192]{1,0:T(8,128)} %bitcast.238, ...), custom_call_target="tpu_custom_call" | custom-call | flops 4529848320 | bytes 15728640 | tf_op jit(solution)/shard_map/within/pallas_call | solution.py:269
  210.1 3.3 %convert_multiply_fusion.refs_5_ = f32[5120,128]{1,0:T(8,128)} fusion(f16[4,1280,128]{2,1,0:T(8,128)(2,1)S(1)} %get-tuple-element.67, f32[5120]{0:T(1024)S(1)} %mul.924), kind=kLoop, calls=%fused_computation.27 | loop fusion | flops 1310720 | bytes 3952640 | tf_op jit(solution)/shard_map/mul | solution.py:180
  213.4 3.2 %convert_multiply_fusion.1.refs_4_ = f32[5120,128]{1,0:T(8,128)} fusion(f16[4,1280,128]{2,1,0:T(8,128)(2,1)S(1)} %get-tuple-element.68, f32[5120]{0:T(1024)S(1)} %mul.920), kind=kLoop, calls=%fused_computation.28 | loop fusion | flops 1310720 | bytes 3952640 | tf_op jit(solution)/shard_map/mul | solution.py:180
  216.6 15.5 %carried.1 = (bf16[192,5120]{1,0:T(8,128)(2,1)}, bf16[192,5120]{1,0:T(8,128)(2,1)}, f32[192,128]{1,0:T(8,128)}, f32[192,128]{1,0:T(8,128)}, f32[192,80]{1,0:T(8,128)}) custom-call(bf16[192,5120]{1,0:T(8,128)(2,1)} %refs_0_.5, bf16[192,5120]{1,0:T(8,128)(2,1)} %refs_1_.5, f32[192,5120]{1,0:T(8,128)} %get-tuple-element.17.refs_2_, ...), custom_call_target="tpu_custom_call" | custom-call | flops 2516582400 | bytes 15728640 | tf_op jit(solution)/shard_map/carried/pallas_call | solution.py:295
  233.8 3.3 %all-to-all-start.3 = ((f32[192,4,20]{0,2,1:T(8,128)}), f32[192,4,20]{0,2,1:T(8,128)S(1)}, u32[]{:S(2)}, u32[]{:S(2)}) async-start(f32[192,4,20]{0,2,1:T(8,128)} %all_to_all.26), calls=%async_computation.3 | async-start | bytes 196608 | tf_op jit(solution)/shard_map/all_to_all | solution.py:306
  238.1 9.1 %all_gather.3 = f32[768,256]{1,0:T(8,128)S(1)} all-gather(f32[192,256]{1,0:T(8,128)S(1)} %pad_maximum_fusion.4), channel_id=1, replica_groups=mesh['ctx'=8,'head'=4] {'head'}, dimensions={0}, use_global_device_ids=true | all-gather | bytes 983040 | tf_op jit(solution)/shard_map/all_gather | solution.py:305
  (265 shorter events, 70.0 us)
Async XLA Ops:
  3.1 8.6 %all-to-all-start = ((f32[4,200,20]{1,2,0:T(8,128)}), f32[4,200,20]{1,2,0:T(8,128)S(1)}, u32[]{:S(2)}, u32[]{:S(2)}) async-start(f32[4,200,20]{1,2,0:T(8,128)} %copy.105), calls=%async_computation | async-start | bytes 196608 | tf_op jit(solution)/shard_map/all_to_all | solution.py:225
  12.0 15.2 %copy-start.26 = (f32[192,80]{0,1:T(8,128)}, f32[192,80]{0,1:T(8,128)S(1)}, u32[]{:S(2)}) copy-start(f32[192,80]{0,1:T(8,128)S(1)} %fusion.32) | copy-start | bytes 184324
  33.7 3.8 %copy-start.27 = (f32[768,20]{0,1:T(8,128)S(1)}, f32[768,20]{0,1:T(8,128)}, u32[]{:S(2)}) copy-start(f32[768,20]{0,1:T(8,128)} %param.10) | copy-start | bytes 184324
  33.7 35.4 %all-to-all-start.1 = ((f16[4,1296,256]{2,1,0:T(8,128)(2,1)}), f16[4,1296,256]{2,1,0:T(8,128)(2,1)S(1)}, u32[]{:S(2)}, u32[]{:S(2)}) async-start(f16[4,1296,256]{2,1,0:T(8,128)(2,1)} %fusion.11), calls=%async_computation.1 | async-start | bytes 5308416 | tf_op jit(solution)/shard_map/all_to_all | solution.py:263
  79.2 11.4 %collective-permute-start.3 = (f16[1296,128]{1,0:T(8,128)(2,1)S(1)}, f16[1296,128]{1,0:T(8,128)(2,1)S(1)}, u32[]{:S(2)}, u32[]{:S(2)}) collective-permute-start(f16[1296,128]{1,0:T(8,128)(2,1)S(1)} %fusion.31), channel_id=1, source_target_pairs={{4,0},{8,4},{12,8},{16,12},{20,16},{24,20},{28,24},{5,1},{9,5},{13... | collective-permute-start | bytes 995336 | tf_op jit(solution)/shard_map/ppermute | solution.py:202
  80.6 17.3 %collective-permute-start = (f16[1296,128]{1,0:T(8,128)(2,1)S(1)}, f16[1296,128]{1,0:T(8,128)(2,1)S(1)}, u32[]{:S(2)}, u32[]{:S(2)}) collective-permute-start(f16[1296,128]{1,0:T(8,128)(2,1)S(1)} %fusion.30), channel_id=1, source_target_pairs={{0,4},{4,8},{8,12},{12,16},{16,20},{20,24},{24,28},{1,5},{5,9},{9,... | collective-permute-start | bytes 995336 | tf_op jit(solution)/shard_map/ppermute | solution.py:202
  90.6 8.0 %copy-start.19 = (f16[1296,128]{1,0:T(8,128)(2,1)}, f16[1296,128]{1,0:T(8,128)(2,1)S(1)}, u32[]{:S(2)}) copy-start(f16[1296,128]{1,0:T(8,128)(2,1)S(1)} %collective-permute-done.3) | copy-start | bytes 995332
  98.9 9.5 %copy-start.30 = (f32[20]{0:T(128)}, f32[20]{0:T(128)S(1)}, u32[]{:S(2)}) copy-start(f32[20]{0:T(128)S(1)} %get-tuple-element.55) | copy-start | bytes 244
  98.9 9.5 %copy-start.32 = (f32[20]{0:T(128)}, f32[20]{0:T(128)S(1)}, u32[]{:S(2)}) copy-start(f32[20]{0:T(128)S(1)} %get-tuple-element.116) | copy-start | bytes 244
  108.4 20.1 %copy-start.31 = (f32[20]{0:T(128)S(1)}, f32[20]{0:T(128)}, u32[]{:S(2)}) copy-start(f32[20]{0:T(128)} %copy-done.30) | copy-start | bytes 244
  108.4 20.1 %copy-start.33 = (f32[20]{0:T(128)S(1)}, f32[20]{0:T(128)}, u32[]{:S(2)}) copy-start(f32[20]{0:T(128)} %copy-done.32) | copy-start | bytes 244
  108.6 11.6 %collective-permute-start.4 = (f16[1296,128]{1,0:T(8,128)(2,1)S(1)}, f16[1296,128]{1,0:T(8,128)(2,1)S(1)}, u32[]{:S(2)}, u32[]{:S(2)}) collective-permute-start(f16[1296,128]{1,0:T(8,128)(2,1)S(1)} %pad_maximum_fusion.2), channel_id=1, source_target_pairs={{8,0},{12,4},{16,8},{20,12},{24,16},{28,20},{9,1},{13,5},{17,9},{2... | collective-permute-start | bytes 995336 | tf_op jit(solution)/shard_map/ppermute | solution.py:202
  110.0 11.5 %collective-permute-start.1 = (f16[1296,128]{1,0:T(8,128)(2,1)S(1)}, f16[1296,128]{1,0:T(8,128)(2,1)S(1)}, u32[]{:S(2)}, u32[]{:S(2)}) collective-permute-start(f16[1296,128]{1,0:T(8,128)(2,1)S(1)} %pad_maximum_fusion), channel_id=1, source_target_pairs={{0,8},{4,12},{8,16},{12,20},{16,24},{20,28},{1,9},{5,13},{9,17},{1... | collective-permute-start | bytes 995336 | tf_op jit(solution)/shard_map/ppermute | solution.py:202
  122.2 8.6 %copy-start.28 = (f32[20]{0:T(128)}, f32[20]{0:T(128)S(1)}, u32[]{:S(2)}) copy-start(f32[20]{0:T(128)S(1)} %get-tuple-element.43) | copy-start | bytes 244
  130.9 7.3 %copy-start.34 = (f16[1,128]{1,0:T(2,128)(2,1)S(1)}, f16[1,128]{1,0:T(2,128)(2,1)}, u32[]{:S(2)}) copy-start(f16[1,128]{1,0:T(2,128)(2,1)} %pad_bitcast_fusion.15) | copy-start | bytes 772
  130.9 7.3 %copy-start.35 = (f16[1,128]{1,0:T(2,128)(2,1)S(1)}, f16[1,128]{1,0:T(2,128)(2,1)}, u32[]{:S(2)}) copy-start(f16[1,128]{1,0:T(2,128)(2,1)} %pad_bitcast_fusion.13) | copy-start | bytes 772
  131.5 6.8 %copy-start.36 = (f16[1,128]{1,0:T(2,128)(2,1)S(1)}, f16[1,128]{1,0:T(2,128)(2,1)}, u32[]{:S(2)}) copy-start(f16[1,128]{1,0:T(2,128)(2,1)} %pad_bitcast_fusion.16) | copy-start | bytes 772
  136.9 18.5 %collective-permute-start.5 = (f16[1296,128]{1,0:T(8,128)(2,1)S(1)}, f16[1296,128]{1,0:T(8,128)(2,1)S(1)}, u32[]{:S(2)}, u32[]{:S(2)}) collective-permute-start(f16[1296,128]{1,0:T(8,128)(2,1)S(1)} %pad_maximum_fusion.3), channel_id=1, source_target_pairs={{16,0},{20,4},{24,8},{28,12},{17,1},{21,5},{25,9},{29,13},{18,2},{... | collective-permute-start | bytes 995336 | tf_op jit(solution)/shard_map/ppermute | solution.py:202
  139.8 21.3 %collective-permute-start.2 = (f16[1296,128]{1,0:T(8,128)(2,1)}, f16[1296,128]{1,0:T(8,128)(2,1)}, u32[]{:S(2)}, u32[]{:S(2)}) collective-permute-start(f16[1296,128]{1,0:T(8,128)(2,1)} %pad_maximum_fusion.1), channel_id=1, source_target_pairs={{0,16},{4,20},{8,24},{12,28},{1,17},{5,21},{9,25},{13,29},{2,18},{... | collective-permute-start | bytes 995336 | tf_op jit(solution)/shard_map/ppermute | solution.py:202
  164.5 3.6 %copy-start.6 = (f32[1,20,64,128]{3,2,1,0:T(8,128)S(1)}, f32[1,20,64,128]{3,2,1,0:T(8,128)}, u32[]{:S(2)}) copy-start(f32[1,20,64,128]{3,2,1,0:T(8,128)} %copy-done.5) | copy-start | bytes 1966084
  164.5 3.6 %copy-start.8 = (f32[1,20,64,128]{3,2,1,0:T(8,128)S(1)}, f32[1,20,64,128]{3,2,1,0:T(8,128)}, u32[]{:S(2)}) copy-start(f32[1,20,64,128]{3,2,1,0:T(8,128)} %copy-done.7) | copy-start | bytes 1966084
  164.5 3.6 %copy-start.10 = (f32[1,20,64,128]{3,2,1,0:T(8,128)S(1)}, f32[1,20,64,128]{3,2,1,0:T(8,128)}, u32[]{:S(2)}) copy-start(f32[1,20,64,128]{3,2,1,0:T(8,128)} %copy-done.9) | copy-start | bytes 1966084
  174.0 35.3 %all-to-all-start.2 = ((f16[4,1296,256]{2,1,0:T(8,128)(2,1)}), f16[4,1296,256]{2,1,0:T(8,128)(2,1)S(1)}, u32[]{:S(2)}, u32[]{:S(2)}) async-start(f16[4,1296,256]{2,1,0:T(8,128)(2,1)} %fusion.13), calls=%async_computation.2 | async-start | bytes 5308416 | tf_op jit(solution)/shard_map/all_to_all | solution.py:263
  233.8 14.3 %all-to-all-start.3 = ((f32[192,4,20]{0,2,1:T(8,128)}), f32[192,4,20]{0,2,1:T(8,128)S(1)}, u32[]{:S(2)}, u32[]{:S(2)}) async-start(f32[192,4,20]{0,2,1:T(8,128)} %all_to_all.26), calls=%async_computation.3 | async-start | bytes 196608 | tf_op jit(solution)/shard_map/all_to_all | solution.py:306
  (23 other events, 41.1 us)

commit v2 on v1

--- a/solution.py
+++ b/solution.py
@@ -1,3 +1,5 @@
+import functools
+
 import jax
 import jax.numpy as jnp
 from jax import lax
@@ -8,7 +10,7 @@
 F32, BF16, F16 = jnp.float32, jnp.bfloat16, jnp.float16
 TINY = 1e-30
 STEP_HEADS = 8
-TAIL_ROWS = 16
+STREAMS = 2
 
 
 def split(value):
@@ -44,12 +46,12 @@
 
 
 def within_kernel(
-    x_ref, dy_ref, cum_ref, cumt_ref, b_ref, c_ref, gain_ref,
-    y_ref, dx_ref, dsc_ref, rows_ref, cols_ref, scores_ref, *, per, width,
+    x_ref, dy_ref, cum_ref, cumt_ref, b_ref, c_ref, gain_ref, *rest, per, width, first,
 ):
-    step = pl.program_id(0)
-
-    @pl.when(step == 0)
+    y_ref, dx_ref, dsc_ref, rows_ref, cols_ref, scores_ref = rest[-6:]
+    step = pl.program_id(0) + first
+
+    @pl.when(step == first)
     def _():
         scores_ref[...] = dot(c_ref[...], b_ref[...], 1, 1)
         dsc_ref[...] = jnp.zeros_like(dsc_ref)
@@ -153,63 +155,40 @@
         )
 
 
-def exponents(value):
-    peak = jnp.max(jnp.abs(value), axis=(-2, -1))
-    return jnp.ceil(jnp.log2(jnp.maximum(peak, TINY)))
-
-
-def lane_row(table, lanes):
-    pad = [(0, 0)] * (table.ndim - 1) + [(0, lanes - table.shape[-1])]
-    return jnp.pad(table, pad)[..., None, :]
-
-
-def pack(value, extra=()):
-    power = exponents(value)
-    lanes = value.shape[-1]
-    rows = (value * jnp.exp2(-power)[..., None, None]).astype(F16)
-    rows = rows.reshape(*value.shape[:-3], -1, lanes)
-    tail = jnp.concatenate([lane_row(t, lanes) for t in (power, *extra)], axis=-2).astype(F16)
-    pad = [(0, 0)] * (tail.ndim - 2) + [(0, TAIL_ROWS - tail.shape[-2]), (0, 0)]
-    return jnp.concatenate([rows, jnp.pad(tail, pad)], axis=-2)
-
-
-def unpack(rows, heads):
-    body, tail = rows[..., :-TAIL_ROWS, :], rows[..., -TAIL_ROWS:, :].astype(F32)
-    body = body.reshape(*body.shape[:-2], heads, -1, body.shape[-1]).astype(F32)
-    tail = tail[..., :heads]
-    return body * jnp.exp2(tail[..., 0, :])[..., None, None], tail
-
-
-def three(value):
-    terms = []
-    for _ in range(3):
-        terms.append(lax.reduce_precision(value, 5, 10))
-        value = value - terms[-1]
-    return terms
-
-
-def chain(total, log_total, axis, backward):
-    count = lax.axis_size(axis)
-    heads = total.shape[0]
-    own, own_log = total, log_total
-    entering, entering_log = jnp.zeros_like(total), jnp.zeros_like(log_total)
+def chain(total, logs, axis, backward):
+    count, mine = logs.shape[0], lax.axis_index(axis)
+    own, entering = total, None
+    own_log, entering_log = logs, jnp.zeros_like(logs)
     reach = 1
     while reach < count:
         pairs = [(i, i + reach) for i in range(count - reach)]
         if backward:
             pairs = [(b, a) for a, b in pairs]
-        sent = pack(own, three(own_log))
-        got, tail = unpack(lax.ppermute(sent, axis, pairs), heads)
-        got_log = tail[1] + tail[2] + tail[3]
-        entering = entering + jnp.exp(entering_log)[:, None, None] * got
-        own = own + jnp.exp(own_log)[:, None, None] * got
-        entering_log, own_log = entering_log + got_log, own_log + got_log
+        got = lax.ppermute(own.astype(F16), axis, pairs).astype(F32)
+
+        def factor(table):
+            row = lax.dynamic_index_in_dim(table, mine, 0, keepdims=False)
+            return jnp.exp(row)[:, None, None]
+
+        scaled = factor(entering_log) * got
+        entering = scaled if entering is None else entering + scaled
+        own = own + factor(own_log) * got
+        blank = jnp.zeros_like(logs[:reach])
+        if backward:
+            moved = jnp.concatenate([own_log[reach:], blank], axis=0)
+        else:
+            moved = jnp.concatenate([blank, own_log[:-reach]], axis=0)
+        entering_log, own_log = entering_log + moved, own_log + moved
         reach *= 2
     return entering
 
 
+def largest(value):
+    return jnp.max(jnp.abs(value)).astype(F32)
+
+
 def shards(signal, cotangent, input_map, output_map, log_decay, skip_gain):
-    members = lax.axis_size("head")
+    members, blocks = lax.axis_size("head"), lax.axis_size("ctx")
     member = lax.axis_index("head")
     length, channels = signal.shape
     own_heads = log_decay.shape[1]
@@ -221,10 +200,23 @@
     lane_block = per * width
 
     by_member = log_decay.reshape(members, length, own_heads)
-    gain_rows = jnp.broadcast_to(skip_gain, (members, 8, own_heads))
+    peaks = jnp.stack([largest(signal), largest(cotangent)])
+    known = jnp.zeros((8, own_heads), F32).at[0].set(skip_gain).at[1:3].set(peaks[:, None])
     rates = lax.all_to_all(
-        jnp.concatenate([by_member, gain_rows], axis=1), "head", split_axis=0, concat_axis=0, tiled=True
+        jnp.concatenate([by_member, jnp.broadcast_to(known, (members, 8, own_heads))], axis=1),
+        "head", split_axis=0, concat_axis=0, tiled=True,
     )
+    logs = jnp.sum(by_member, axis=1)
+    maps_peak = jnp.stack([largest(input_map), largest(output_map)])
+    bounds = jnp.max(rates[:, length + 1 : length + 3, 0], axis=0) * maps_peak
+    told = jnp.stack([jnp.sum(logs, axis=0), *jnp.broadcast_to(bounds[:, None], (2, own_heads))])
+    told = lax.all_to_all(
+        jnp.broadcast_to(told, (blocks, 3, own_heads)), "ctx", split_axis=0, concat_axis=0, tiled=True
+    )
+    block_logs = told[:, 0]
+    terms = blocks * members * length
+    limits = jnp.maximum(jnp.max(told[:, 1:, 0], axis=0) * terms, TINY)
+    grow = jnp.exp2(14.0 - jnp.ceil(jnp.log2(limits)))
     rates = jnp.swapaxes(rates, 0, 1).reshape(length + 8, heads)
     decay, gains = rates[:length], rates[length]
     into = lax.dynamic_slice_in_dim(input_map, member * length, length, 0)
@@ -258,38 +250,64 @@
         [sd((channels, state), F32)] * 2, flops=8 * length * channels * state,
     )(signal, cotangent, cum, into, outof)
 
+    shape = (members, own_heads, width, state)
+    piece = own_heads // STREAMS
+    pieces = [slice(i * piece, (i + 1) * piece) for i in range(STREAMS)]
+
     def swap(f, b):
-        both = jnp.concatenate([pack(f), pack(b)], axis=-1)
+        both = jnp.concatenate([f.astype(F16), b.astype(F16)], axis=-1)
+        both = both.reshape(members, piece * width, 2 * state)
         both = lax.all_to_all(both, "head", split_axis=0, concat_axis=0, tiled=True)
-        return [unpack(half, own_heads)[0] for half in (both[..., :state], both[..., state:])]
-
-    shape = (members, own_heads, width, state)
-    parts_f, parts_b = swap(own_state.reshape(shape), own_seed.reshape(shape))
-
-    y_local, dx_local, dscores, rows, cols = call(
-        within_kernel, "within",
-        [wide, wide, whole(length, heads), pl.BlockSpec((per, length), lambda k: (k, 0))] + maps
-        + [pl.BlockSpec((1, lane_block), lambda k: (0, k))],
-        [wide, wide, whole(length, length), whole(length, heads),
-         pl.BlockSpec((per, length), lambda k: (k, 0))],
-        [sd((length, channels), F32)] * 2
-        + [sd((length, length), F32), sd((length, heads), F32), sd((heads, length), F32)],
-        scratch=[pltpu.VMEM((length, length), F32)], flops=24 * length * length * channels,
-    )(signal, cotangent, cum, cum_t, into, outof, gain_row)
-
-    logs = jnp.sum(by_member, axis=1)
-    keep = jnp.exp(logs)[:, :, None, None]
-    group_f, group_b = parts_f[0], parts_b[-1]
-    for s in range(1, members):
-        group_f = keep[s] * group_f + parts_f[s]
-        group_b = keep[members - 1 - s] * group_b + parts_b[members - 1 - s]
-    group_log = jnp.sum(logs, axis=0)
-    list_f = [chain(group_f, group_log, "ctx", False)]
-    list_b = [chain(group_b, group_log, "ctx", True)]
-    for s in range(members - 1):
-        list_f.append(keep[s] * list_f[-1] + parts_f[s])
-        list_b.append(keep[members - 1 - s] * list_b[-1] + parts_b[members - 1 - s])
-    e_all, l_all = swap(jnp.stack(list_f), jnp.stack(list_b[::-1]))
+        both = both.reshape(members, piece, width, 2 * state)
+        return both[..., :state], both[..., state:]
+
+    sums_f, sums_b = own_state.reshape(shape), own_seed.reshape(shape)
+    arrived = [swap(sums_f[:, at] * grow[0], sums_b[:, at] * grow[1]) for at in pieces]
+
+    def within(first, last, earlier):
+        wide_at = pl.BlockSpec((length, lane_block), lambda k: (0, k + first))
+        rows_at = pl.BlockSpec((per, length), lambda k: (k + first, 0))
+        gain_at = pl.BlockSpec((1, lane_block), lambda k: (0, k + first))
+        return pl.pallas_call(
+            functools.partial(within_kernel, per=per, width=width, first=first),
+            grid=(last - first,),
+            in_specs=[wide_at, wide_at, whole(length, heads), rows_at] + maps + [gain_at]
+            + [pl.BlockSpec(memory_space=pl.ANY)] * len(earlier),
+            out_specs=[wide_at, wide_at, whole(length, length), whole(length, heads), rows_at],
+            out_shape=[sd((length, channels), F32)] * 2
+            + [sd((length, length), F32), sd((length, heads), F32), sd((heads, length), F32)],
+            scratch_shapes=[pltpu.VMEM((length, length), F32)], name="within",
+            input_output_aliases=dict(zip((7, 8, 9), (0, 1, 4))) if earlier else {},
+            cost_estimate=pl.CostEstimate(
+                flops=24 * length * length * channels, transcendentals=0,
+                bytes_accessed=16 * length * channels,
+            ),
+        )(signal, cotangent, cum, cum_t, into, outof, gain_row, *earlier)
+
+    y_half, dx_half, dscores_a, rows_a, cols_half = within(0, steps // 2, ())
+    arrived[0], rows_a = lax.optimization_barrier((arrived[0], rows_a))
+
+    homes, ready = [], None
+    for at, (parts_f, parts_b) in zip(pieces, arrived):
+        if ready is not None:
+            parts_f, parts_b, ready = lax.optimization_barrier((parts_f, parts_b, ready))
+        parts_f, parts_b = parts_f.astype(F32), parts_b.astype(F32)
+        keep = jnp.exp(logs[:, at])[:, :, None, None]
+        group_f, group_b = parts_f[0], parts_b[-1]
+        for s in range(1, members):
+            group_f = keep[s] * group_f + parts_f[s]
+            group_b = keep[members - 1 - s] * group_b + parts_b[members - 1 - s]
+        list_f = [chain(group_f, block_logs[:, at], "ctx", False)]
+        list_b = [chain(group_b, block_logs[:, at], "ctx", True)]
+        ready = list_f[0][0, :8] + list_b[0][0, :8]
+        for s in range(members - 1):
+            list_f.append(keep[s] * list_f[-1] + parts_f[s])
+            list_b.append(keep[members - 1 - s] * list_b[-1] + parts_b[members - 1 - s])
+        homes.append(swap(jnp.stack(list_f), jnp.stack(list_b[::-1])))
+    y_local, dx_local, dscores_b, rows_b, cols = within(steps // 2, steps, (y_half, dx_half, cols_half))
+    dscores, rows = dscores_a + dscores_b, rows_a + rows_b
+    e_all = jnp.concatenate([h[0] for h in homes], axis=1).astype(F32) / grow[0]
+    l_all = jnp.concatenate([h[1] for h in homes], axis=1).astype(F32) / grow[1]
     e_all, l_all = e_all.reshape(channels, state), l_all.reshape(channels, state)
 
     scan_out, grad_signal, grad_in, grad_out, grad_decay = call(

time: 251 us -> 251 us (level)
  starting transfers between devices: 34.2 us -> 60.3 us
  other arithmetic: 57.5 us -> 34.4 us
  local copies, waits for them, and re-layouts: 28.5 us -> 15.4 us
  waiting for transfers between devices: 62.5 us -> 71.1 us
    all_to_all x2 -> x4, waiting for transfers between devices: 30.6 us -> 42.9 us  [swap(): both = lax.all_to_all(both, 'head', split_axis=0, concat_axis=0, tiled=True)]
    convert_element_type x17 -> x18, other arithmetic: 21.1 us -> 8.91 us  [the longest x12 3.75 us: chain(): got = lax.ppermute(own.astype(F16), axis, pairs).astype(F32)]
    ppermute x6 -> x12, starting transfers between devices: 19.2 us -> 30.6 us  [chain(): got = lax.ppermute(own.astype(F16), axis, pairs).astype(F32)]
    all_to_all x2 -> x4, starting transfers between devices: 7.44 us -> 15.9 us  [swap(): both = lax.all_to_all(both, 'head', split_axis=0, concat_axis=0, tiled=True)]
    all_to_all x1 -> x2, starting transfers between devices: 4.26 us -> 10.6 us  [the longest x1 6.29 us: shards(): lax.all_to_all(jnp.broadcast_to(told, (blocks, 3, own_heads)), 'ctx', spl...]
    add x4 -> x6, other arithmetic: 7.85 us -> 1.74 us  [the longest x1 1.63 us: shards(): dscores, rows = (dscores_a + dscores_b, rows_a + rows_b)]
    ppermute x6 -> x12, waiting for transfers between devices: 29.1 us -> 23 us  [chain(): got = lax.ppermute(own.astype(F16), axis, pairs).astype(F32)]
    mul x4 -> x1, other arithmetic: 7.08 us -> 1.37 us  [shards(): bounds = jnp.max(rates[:, length + 1:length + 3, 0], axis=0) * maps_peak]
  transfers between devices with their start and end apart: 10 -> 19, of which waited for: 8 -> 10; matrix products, arithmetic and copies ran while one was open for 5% -> 9% of each run, Pallas kernels for 11% -> 17%
where the time goes in v2:
time: 251 us; the launch traced here: 250 us
  waiting for transfers between devices  71.1 us (28%)
  starting transfers between devices  60.3 us (24%)
  Pallas kernels  57.7 us (23%)
  other arithmetic  34.4 us (14%)
  local copies, waits for them, and re-layouts  15.4 us (6%)
  blocking collectives  9.02 us (4%)
    all_to_all x4, waiting for transfers between devices, swap(): both = lax.all_to_all(both, 'head', split_axis=0, concat_axis=0, tiled=True)  42.9 us
    ppermute x12, starting transfers between devices, chain(): got = lax.ppermute(own.astype(F16), axis, pairs).astype(F32)  30.6 us
    pallas_call x2, Pallas kernels, within(): pl.pallas_call(functools.partial(within_kernel, per=per, width=width, fir...  30.4 us
    ppermute x12, waiting for transfers between devices, chain(): got = lax.ppermute(own.astype(F16), axis, pairs).astype(F32)  23 us
    all_to_all x4, starting transfers between devices, swap(): both = lax.all_to_all(both, 'head', split_axis=0, concat_axis=0, tiled=True)  15.9 us
    pallas_call x1, Pallas kernels, shards(): call(carried_kernel, 'carried', [wide, wide, wide, wide, tall, tall, whol...  15.5 us
    pallas_call x1, Pallas kernels, shards(): call(states_kernel, 'states', [wide, wide, whole(length, heads)] + maps,...  11.8 us
    all_gather x1, blocking collectives, shards(): lax.all_gather(jnp.concatenate([grad_in, grad_out], axis=1), 'head', tile...  9.02 us
  transfers between devices with their start and end apart: 19, of which 10 were waited for; matrix products, arithmetic and copies ran while one was open for 9% of the time, Pallas kernels for 17%

profile of v2, /device:TPU:0, one launch (start us, length us, event | category | flops | bytes accessed | tf_op | source)
XLA Modules:
  0.0 249.6 jit_solution(10085383463221836614)
XLA Ops:
  6.6 4.3 %all-to-all-start = ((f32[4,200,20]{1,2,0:T(8,128)}), f32[4,200,20]{1,2,0:T(8,128)S(1)}, u32[]{:S(2)}, u32[]{:S(2)}) async-start(f32[4,200,20]{1,2,0:T(8,128)} %copy.48), calls=%async_computation | async-start | bytes 196608 | tf_op jit(solution)/shard_map/all_to_all | solution.py:205
  21.3 6.3 %all-to-all-start.1 = ((f32[8,3,20]{2,1,0:T(4,128)}), f32[8,3,20]{2,1,0:T(4,128)S(1)}, u32[]{:S(2)}, u32[]{:S(2)}) async-start(f32[8,3,20]{2,1,0:T(4,128)} %broadcast_in_dim.14), calls=%async_computation.1 | async-start | bytes 32768 | tf_op jit(solution)/shard_map/all_to_all | solution.py:213
  27.6 15.2 %within.2 = (f32[192,5120]{1,0:T(8,128)}, f32[192,5120]{1,0:T(8,128)}, f32[192,192]{1,0:T(8,128)}, f32[192,80]{1,0:T(8,128)}, f32[80,192]{1,0:T(8,128)}) custom-call(bf16[192,5120]{1,0:T(8,128)(2,1)} %refs_0_.3, bf16[192,5120]{1,0:T(8,128)(2,1)} %refs_1_.3, f32[192,80]{1,0:T(8,128)} %copy.50.cum_ref.refs_2_.refs_6_, f32[80,192]{1,0:T(8,128)} %bitcast.237, ...), custom_call_target="tpu_custom_call" | custom-call | flops 4529848320 | bytes 15728640 | tf_op jit(solution)/shard_map/within/pallas_call | solution.py:271
  42.8 11.8 %states.1 = (f32[5120,128]{1,0:T(8,128)}, f32[5120,128]{1,0:T(8,128)}) custom-call(bf16[192,5120]{1,0:T(8,128)(2,1)} %refs_0_.3, bf16[192,5120]{1,0:T(8,128)(2,1)} %refs_1_.3, f32[192,80]{1,0:T(8,128)} %copy.50.cum_ref.refs_2_.refs_6_, bf16[192,128]{1,0:T(8,128)(2,1)} %get-tuple-element.150.b_ref.refs_3_.refs_7_, ...), custom_call_target="tpu_custom_call" | custom-call | flops 1006632960 | bytes 15728640 | tf_op jit(solution)/shard_map/states/pallas_call | solution.py:248
  55.4 2.8 %fusion.2 = (f16[4,10,64,128]{3,2,1,0:T(8,128)(2,1)S(1)}, f16[4,10,64,128]{3,2,1,0:T(8,128)(2,1)S(1)}) fusion(f32[4,20,64,128]{3,2,1,0:T(8,128)} %bitcast.217, f32[]{:T(128)} %bitcast.14), kind=kLoop, calls=%fused_computation.9 | loop fusion | flops 1310720 | bytes 3932164 | tf_op jit(solution)/shard_map/convert_element_type | solution.py:258
  60.6 3.5 %all-to-all-start.4 = ((f16[4,640,256]{2,1,0:T(8,128)(2,1)}), f16[4,640,256]{2,1,0:T(8,128)(2,1)S(1)}, u32[]{:S(2)}, u32[]{:S(2)}) async-start(f16[4,640,256]{2,1,0:T(8,128)(2,1)} %bitcast.42), calls=%async_computation.4 | async-start | bytes 2621440 | tf_op jit(solution)/shard_map/all_to_all | solution.py:260
  66.1 15.3 %all-to-all-done.4 = f16[4,640,256]{2,1,0:T(8,128)(2,1)S(1)} async-done(((f16[4,640,256]{2,1,0:T(8,128)(2,1)}), f16[4,640,256]{2,1,0:T(8,128)(2,1)S(1)}, u32[]{:S(2)}, u32[]{:S(2)}) %all-to-all-start.4) | async-done | bytes 1310752 | tf_op jit(solution)/shard_map/all_to_all | solution.py:260
  81.4 4.3 %all-to-all-start.2 = ((f16[4,640,256]{2,1,0:T(8,128)(2,1)}), f16[4,640,256]{2,1,0:T(8,128)(2,1)}, u32[]{:S(2)}, u32[]{:S(2)}) async-start(f16[4,640,256]{2,1,0:T(8,128)(2,1)} %bitcast.15), calls=%async_computation.2 | async-start | bytes 2621440 | tf_op jit(solution)/shard_map/all_to_all | solution.py:260
  89.0 14.1 %all-to-all-done.2 = f16[4,640,256]{2,1,0:T(8,128)(2,1)} async-done(((f16[4,640,256]{2,1,0:T(8,128)(2,1)}), f16[4,640,256]{2,1,0:T(8,128)(2,1)}, u32[]{:S(2)}, u32[]{:S(2)}) %all-to-all-start.2) | async-done | bytes 1310752 | tf_op jit(solution)/shard_map/all_to_all | solution.py:260
  108.0 4.9 %collective-permute-done.3 = f16[10,64,128]{2,1,0:T(8,128)(2,1)S(1)} collective-permute-done((f16[10,64,128]{2,1,0:T(8,128)(2,1)S(1)}, f16[10,64,128]{2,1,0:T(8,128)(2,1)S(1)}, u32[]{:S(2)}, u32[]{:S(2)}) %collective-permute-start.3) | collective-permute-done | bytes 163872 | tf_op jit(solution)/shard_map/ppermute | solution.py:167
  114.3 4.4 %collective-permute-done.10 = f16[10,64,128]{2,1,0:T(8,128)(2,1)S(1)} collective-permute-done((f16[10,64,128]{2,1,0:T(8,128)(2,1)S(1)}, f16[10,64,128]{2,1,0:T(8,128)(2,1)S(1)}, u32[]{:S(2)}, u32[]{:S(2)}) %collective-permute-start.10) | collective-permute-done | bytes 163872 | tf_op jit(solution)/shard_map/ppermute | solution.py:167
  122.6 11.4 %collective-permute-done.11 = f16[10,64,128]{2,1,0:T(8,128)(2,1)S(1)} collective-permute-done((f16[10,64,128]{2,1,0:T(8,128)(2,1)S(1)}, f16[10,64,128]{2,1,0:T(8,128)(2,1)S(1)}, u32[]{:S(2)}, u32[]{:S(2)}) %collective-permute-start.11) | collective-permute-done | bytes 163872 | tf_op jit(solution)/shard_map/ppermute | solution.py:167
  140.6 4.3 %collective-permute-start.7 = (f16[10,64,128]{2,1,0:T(8,128)(2,1)S(1)}, f16[10,64,128]{2,1,0:T(8,128)(2,1)S(1)}, u32[]{:S(2)}, u32[]{:S(2)}) collective-permute-start(f16[10,64,128]{2,1,0:T(8,128)(2,1)S(1)} %fusion.25), channel_id=1, source_target_pairs={{0,8},{4,12},{8,16},{12,20},{16,24},{20,28},{1,9},{5,13},{9,17},{1... | collective-permute-start | bytes 491528 | tf_op jit(solution)/shard_map/ppermute | solution.py:167
  145.1 3.3 %collective-permute-start.1 = (f16[10,64,128]{2,1,0:T(8,128)(2,1)S(1)}, f16[10,64,128]{2,1,0:T(8,128)(2,1)S(1)}, u32[]{:S(2)}, u32[]{:S(2)}) collective-permute-start(f16[10,64,128]{2,1,0:T(8,128)(2,1)S(1)} %fusion.27), channel_id=1, source_target_pairs={{0,8},{4,12},{8,16},{12,20},{16,24},{20,28},{1,9},{5,13},{9,17},{1... | collective-permute-start | bytes 491528 | tf_op jit(solution)/shard_map/ppermute | solution.py:167
  148.6 7.9 %collective-permute-start.8 = (f16[10,64,128]{2,1,0:T(8,128)(2,1)S(1)}, f16[10,64,128]{2,1,0:T(8,128)(2,1)S(1)}, u32[]{:S(2)}, u32[]{:S(2)}) collective-permute-start(f16[10,64,128]{2,1,0:T(8,128)(2,1)S(1)} %fusion.15), channel_id=1, source_target_pairs={{0,16},{4,20},{8,24},{12,28},{1,17},{5,21},{9,25},{13,29},{2,18},{... | collective-permute-start | bytes 491528 | tf_op jit(solution)/shard_map/ppermute | solution.py:167
  157.4 3.6 %collective-permute-start.2 = (f16[10,64,128]{2,1,0:T(8,128)(2,1)}, f16[10,64,128]{2,1,0:T(8,128)(2,1)}, u32[]{:S(2)}, u32[]{:S(2)}) collective-permute-start(f16[10,64,128]{2,1,0:T(8,128)(2,1)} %fusion.7), channel_id=1, source_target_pairs={{0,16},{4,20},{8,24},{12,28},{1,17},{5,21},{9,25},{13,29},{2,18},{... | collective-permute-start | bytes 491528 | tf_op jit(solution)/shard_map/ppermute | solution.py:167
  163.0 4.5 %all-to-all-start.5 = ((f16[4,640,256]{2,1,0:T(8,128)(2,1)}), f16[4,640,256]{2,1,0:T(8,128)(2,1)}, u32[]{:S(2)}, u32[]{:S(2)}) async-start(f16[4,640,256]{2,1,0:T(8,128)(2,1)} %maximum_maximum_fusion.1), calls=%async_computation.5 | async-start | bytes 2621440 | tf_op jit(solution)/shard_map/all_to_all | solution.py:260
  171.2 13.6 %all-to-all-done.5 = f16[4,640,256]{2,1,0:T(8,128)(2,1)} async-done(((f16[4,640,256]{2,1,0:T(8,128)(2,1)}), f16[4,640,256]{2,1,0:T(8,128)(2,1)}, u32[]{:S(2)}, u32[]{:S(2)}) %all-to-all-start.5) | async-done | bytes 1310752 | tf_op jit(solution)/shard_map/all_to_all | solution.py:260
  184.8 3.5 %all-to-all-start.3 = ((f16[4,640,256]{2,1,0:T(8,128)(2,1)}), f16[4,640,256]{2,1,0:T(8,128)(2,1)S(1)}, u32[]{:S(2)}, u32[]{:S(2)}) async-start(f16[4,640,256]{2,1,0:T(8,128)(2,1)} %maximum_maximum_fusion), calls=%async_computation.3 | async-start | bytes 2621440 | tf_op jit(solution)/shard_map/all_to_all | solution.py:260
  188.4 15.2 %within.3 = (f32[192,5120]{1,0:T(8,128)}, f32[192,5120]{1,0:T(8,128)}, f32[192,192]{1,0:T(8,128)}, f32[192,80]{1,0:T(8,128)}, f32[80,192]{1,0:T(8,128)}) custom-call(bf16[192,5120]{1,0:T(8,128)(2,1)} %refs_0_.3, bf16[192,5120]{1,0:T(8,128)(2,1)} %refs_1_.3, ...), custom_call_target="tpu_custom_call", output_to_operand_aliasing={{0}: (7, {}), {1}: (8, {}), {4}: (9, {})} | custom-call | flops 4529848320 | bytes 15728640 | tf_op jit(solution)/shard_map/within/pallas_call | solution.py:271
  214.9 15.5 %carried.1 = (bf16[192,5120]{1,0:T(8,128)(2,1)}, bf16[192,5120]{1,0:T(8,128)(2,1)}, f32[192,128]{1,0:T(8,128)}, f32[192,128]{1,0:T(8,128)}, f32[192,80]{1,0:T(8,128)}) custom-call(bf16[192,5120]{1,0:T(8,128)(2,1)} %refs_0_.3, bf16[192,5120]{1,0:T(8,128)(2,1)} %refs_1_.3, f32[192,5120]{1,0:T(8,128)} %get-tuple-element.54.refs_2_, ...), custom_call_target="tpu_custom_call" | custom-call | flops 2516582400 | bytes 15728640 | tf_op jit(solution)/shard_map/carried/pallas_call | solution.py:313
  231.4 9.0 %all_gather.3 = f32[768,256]{1,0:T(8,128)S(1)} all-gather(f32[192,256]{1,0:T(8,128)S(1)} %pad_maximum_fusion.2), channel_id=1, replica_groups=mesh['ctx'=8,'head'=4] {'head'}, dimensions={0}, use_global_device_ids=true | all-gather | bytes 983040 | tf_op jit(solution)/shard_map/all_gather | solution.py:323
  241.2 3.3 %all-to-all-start.6 = ((f32[192,4,20]{0,2,1:T(8,128)}), f32[192,4,20]{0,2,1:T(8,128)S(1)}, u32[]{:S(2)}, u32[]{:S(2)}) async-start(f32[192,4,20]{0,2,1:T(8,128)} %all_to_all.38), calls=%async_computation.6 | async-start | bytes 196608 | tf_op jit(solution)/shard_map/all_to_all | solution.py:324
  245.4 3.3 %all-to-all-done.6 = f32[192,4,20]{0,2,1:T(8,128)S(1)} async-done(((f32[192,4,20]{0,2,1:T(8,128)}), f32[192,4,20]{0,2,1:T(8,128)S(1)}, u32[]{:S(2)}, u32[]{:S(2)}) %all-to-all-start.6) | async-done | bytes 61472 | tf_op jit(solution)/shard_map/all_to_all | solution.py:324
  (146 shorter events, 62.8 us)
Async XLA Ops:
  6.6 8.6 %all-to-all-start = ((f32[4,200,20]{1,2,0:T(8,128)}), f32[4,200,20]{1,2,0:T(8,128)S(1)}, u32[]{:S(2)}, u32[]{:S(2)}) async-start(f32[4,200,20]{1,2,0:T(8,128)} %copy.48), calls=%async_computation | async-start | bytes 196608 | tf_op jit(solution)/shard_map/all_to_all | solution.py:205
  15.6 12.1 %copy-start.6 = (f32[192,80]{0,1:T(8,128)}, f32[192,80]{0,1:T(8,128)S(1)}, u32[]{:S(2)}) copy-start(f32[192,80]{0,1:T(8,128)S(1)} %fusion.28) | copy-start | bytes 184324
  21.3 33.3 %all-to-all-start.1 = ((f32[8,3,20]{2,1,0:T(4,128)}), f32[8,3,20]{2,1,0:T(4,128)S(1)}, u32[]{:S(2)}, u32[]{:S(2)}) async-start(f32[8,3,20]{2,1,0:T(4,128)} %broadcast_in_dim.14), calls=%async_computation.1 | async-start | bytes 32768 | tf_op jit(solution)/shard_map/all_to_all | solution.py:213
  60.6 20.8 %all-to-all-start.4 = ((f16[4,640,256]{2,1,0:T(8,128)(2,1)}), f16[4,640,256]{2,1,0:T(8,128)(2,1)S(1)}, u32[]{:S(2)}, u32[]{:S(2)}) async-start(f16[4,640,256]{2,1,0:T(8,128)(2,1)} %bitcast.42), calls=%async_computation.4 | async-start | bytes 2621440 | tf_op jit(solution)/shard_map/all_to_all | solution.py:260
  81.4 21.6 %all-to-all-start.2 = ((f16[4,640,256]{2,1,0:T(8,128)(2,1)}), f16[4,640,256]{2,1,0:T(8,128)(2,1)}, u32[]{:S(2)}, u32[]{:S(2)}) async-start(f16[4,640,256]{2,1,0:T(8,128)(2,1)} %bitcast.15), calls=%async_computation.2 | async-start | bytes 2621440 | tf_op jit(solution)/shard_map/all_to_all | solution.py:260
  87.7 18.7 %collective-permute-start.9 = (f16[10,64,128]{2,1,0:T(8,128)(2,1)S(1)}, f16[10,64,128]{2,1,0:T(8,128)(2,1)S(1)}, u32[]{:S(2)}, u32[]{:S(2)}) collective-permute-start(f16[10,64,128]{2,1,0:T(8,128)(2,1)S(1)} %get-tuple-element.95), channel_id=1, source_target_pairs={{4,0},{8,4},{12,8},{16,12},{20,16},{24,20},{28,24},{5,1},{9,5},{13... | collective-permute-start | bytes 491528 | tf_op jit(solution)/shard_map/ppermute | solution.py:167
  104.8 31.4 %copy-start.1 = (f32[4,10,64,128]{3,2,1,0:T(8,128)}, f32[4,10,64,128]{3,2,1,0:T(8,128)S(1)}, u32[]{:S(2)}) copy-start(f32[4,10,64,128]{3,2,1,0:T(8,128)S(1)} %convert_element_type.121) | copy-start | bytes 3932164
  105.1 7.8 %collective-permute-start.3 = (f16[10,64,128]{2,1,0:T(8,128)(2,1)S(1)}, f16[10,64,128]{2,1,0:T(8,128)(2,1)S(1)}, u32[]{:S(2)}, u32[]{:S(2)}) collective-permute-start(f16[10,64,128]{2,1,0:T(8,128)(2,1)S(1)} %get-tuple-element.87), channel_id=1, source_target_pairs={{4,0},{8,4},{12,8},{16,12},{20,16},{24,20},{28,24},{5,1},{9,5},{13... | collective-permute-start | bytes 491528 | tf_op jit(solution)/shard_map/ppermute | solution.py:167
  106.5 27.5 %copy-start.3 = (f32[4,10,64,128]{3,2,1,0:T(8,128)S(1)}, f32[4,10,64,128]{3,2,1,0:T(8,128)}, u32[]{:S(2)}) copy-start(f32[4,10,64,128]{3,2,1,0:T(8,128)} %convert_element_type.137) | copy-start | bytes 3932164
  106.5 12.2 %collective-permute-start.10 = (f16[10,64,128]{2,1,0:T(8,128)(2,1)S(1)}, f16[10,64,128]{2,1,0:T(8,128)(2,1)S(1)}, u32[]{:S(2)}, u32[]{:S(2)}) collective-permute-start(f16[10,64,128]{2,1,0:T(8,128)(2,1)S(1)} %fusion.24), channel_id=1, source_target_pairs={{8,0},{12,4},{16,8},{20,12},{24,16},{28,20},{9,1},{13,5},{17,9},{2... | collective-permute-start | bytes 491528 | tf_op jit(solution)/shard_map/ppermute | solution.py:167
  113.0 8.1 %collective-permute-start.4 = (f16[10,64,128]{2,1,0:T(8,128)(2,1)S(1)}, f16[10,64,128]{2,1,0:T(8,128)(2,1)S(1)}, u32[]{:S(2)}, u32[]{:S(2)}) collective-permute-start(f16[10,64,128]{2,1,0:T(8,128)(2,1)S(1)} %fusion.26), channel_id=1, source_target_pairs={{8,0},{12,4},{16,8},{20,12},{24,16},{28,20},{9,1},{13,5},{17,9},{2... | collective-permute-start | bytes 491528 | tf_op jit(solution)/shard_map/ppermute | solution.py:167
  118.9 15.1 %collective-permute-start.11 = (f16[10,64,128]{2,1,0:T(8,128)(2,1)S(1)}, f16[10,64,128]{2,1,0:T(8,128)(2,1)S(1)}, u32[]{:S(2)}, u32[]{:S(2)}) collective-permute-start(f16[10,64,128]{2,1,0:T(8,128)(2,1)S(1)} %fusion.19), channel_id=1, source_target_pairs={{16,0},{20,4},{24,8},{28,12},{17,1},{21,5},{25,9},{29,13},{18,2},{... | collective-permute-start | bytes 491528 | tf_op jit(solution)/shard_map/ppermute | solution.py:167
  121.3 14.9 %collective-permute-start.5 = (f16[10,64,128]{2,1,0:T(8,128)(2,1)S(1)}, f16[10,64,128]{2,1,0:T(8,128)(2,1)S(1)}, u32[]{:S(2)}, u32[]{:S(2)}) collective-permute-start(f16[10,64,128]{2,1,0:T(8,128)(2,1)S(1)} %fusion.11), channel_id=1, source_target_pairs={{16,0},{20,4},{24,8},{28,12},{17,1},{21,5},{25,9},{29,13},{18,2},{... | collective-permute-start | bytes 491528 | tf_op jit(solution)/shard_map/ppermute | solution.py:167
  134.5 6.0 %collective-permute-start.6 = (f16[10,64,128]{2,1,0:T(8,128)(2,1)S(1)}, f16[10,64,128]{2,1,0:T(8,128)(2,1)S(1)}, u32[]{:S(2)}, u32[]{:S(2)}) collective-permute-start(f16[10,64,128]{2,1,0:T(8,128)(2,1)S(1)} %get-tuple-element.91), channel_id=1, source_target_pairs={{0,4},{4,8},{8,12},{12,16},{16,20},{20,24},{24,28},{1,5},{5,9},{9,... | collective-permute-start | bytes 491528 | tf_op jit(solution)/shard_map/ppermute | solution.py:167
  137.3 7.7 %collective-permute-start = (f16[10,64,128]{2,1,0:T(8,128)(2,1)S(1)}, f16[10,64,128]{2,1,0:T(8,128)(2,1)S(1)}, u32[]{:S(2)}, u32[]{:S(2)}) collective-permute-start(f16[10,64,128]{2,1,0:T(8,128)(2,1)S(1)} %get-tuple-element.83), channel_id=1, source_target_pairs={{0,4},{4,8},{8,12},{12,16},{16,20},{20,24},{24,28},{1,5},{5,9},{9,... | collective-permute-start | bytes 491528 | tf_op jit(solution)/shard_map/ppermute | solution.py:167
  140.6 7.8 %collective-permute-start.7 = (f16[10,64,128]{2,1,0:T(8,128)(2,1)S(1)}, f16[10,64,128]{2,1,0:T(8,128)(2,1)S(1)}, u32[]{:S(2)}, u32[]{:S(2)}) collective-permute-start(f16[10,64,128]{2,1,0:T(8,128)(2,1)S(1)} %fusion.25), channel_id=1, source_target_pairs={{0,8},{4,12},{8,16},{12,20},{16,24},{20,28},{1,9},{5,13},{9,17},{1... | collective-permute-start | bytes 491528 | tf_op jit(solution)/shard_map/ppermute | solution.py:167
  145.1 11.4 %collective-permute-start.1 = (f16[10,64,128]{2,1,0:T(8,128)(2,1)S(1)}, f16[10,64,128]{2,1,0:T(8,128)(2,1)S(1)}, u32[]{:S(2)}, u32[]{:S(2)}) collective-permute-start(f16[10,64,128]{2,1,0:T(8,128)(2,1)S(1)} %fusion.27), channel_id=1, source_target_pairs={{0,8},{4,12},{8,16},{12,20},{16,24},{20,28},{1,9},{5,13},{9,17},{1... | collective-permute-start | bytes 491528 | tf_op jit(solution)/shard_map/ppermute | solution.py:167
  148.6 12.3 %collective-permute-start.8 = (f16[10,64,128]{2,1,0:T(8,128)(2,1)S(1)}, f16[10,64,128]{2,1,0:T(8,128)(2,1)S(1)}, u32[]{:S(2)}, u32[]{:S(2)}) collective-permute-start(f16[10,64,128]{2,1,0:T(8,128)(2,1)S(1)} %fusion.15), channel_id=1, source_target_pairs={{0,16},{4,20},{8,24},{12,28},{1,17},{5,21},{9,25},{13,29},{2,18},{... | collective-permute-start | bytes 491528 | tf_op jit(solution)/shard_map/ppermute | solution.py:167
  157.4 10.2 %collective-permute-start.2 = (f16[10,64,128]{2,1,0:T(8,128)(2,1)}, f16[10,64,128]{2,1,0:T(8,128)(2,1)}, u32[]{:S(2)}, u32[]{:S(2)}) collective-permute-start(f16[10,64,128]{2,1,0:T(8,128)(2,1)} %fusion.7), channel_id=1, source_target_pairs={{0,16},{4,20},{8,24},{12,28},{1,17},{5,21},{9,25},{13,29},{2,18},{... | collective-permute-start | bytes 491528 | tf_op jit(solution)/shard_map/ppermute | solution.py:167
  163.0 21.8 %all-to-all-start.5 = ((f16[4,640,256]{2,1,0:T(8,128)(2,1)}), f16[4,640,256]{2,1,0:T(8,128)(2,1)}, u32[]{:S(2)}, u32[]{:S(2)}) async-start(f16[4,640,256]{2,1,0:T(8,128)(2,1)} %maximum_maximum_fusion.1), calls=%async_computation.5 | async-start | bytes 2621440 | tf_op jit(solution)/shard_map/all_to_all | solution.py:260
  184.8 24.7 %all-to-all-start.3 = ((f16[4,640,256]{2,1,0:T(8,128)(2,1)}), f16[4,640,256]{2,1,0:T(8,128)(2,1)S(1)}, u32[]{:S(2)}, u32[]{:S(2)}) async-start(f16[4,640,256]{2,1,0:T(8,128)(2,1)} %maximum_maximum_fusion), calls=%async_computation.3 | async-start | bytes 2621440 | tf_op jit(solution)/shard_map/all_to_all | solution.py:260
  188.3 16.2 %copy-start.10 = (f32[192,192]{1,0:T(8,128)S(1)}, f32[192,192]{1,0:T(8,128)}, u32[]{:S(2)}) copy-start(f32[192,192]{1,0:T(8,128)} %get-tuple-element.63) | copy-start | bytes 442372
  188.4 17.9 %copy-start.11 = (f32[192,80]{1,0:T(8,128)S(1)}, f32[192,80]{1,0:T(8,128)}, u32[]{:S(2)}) copy-start(f32[192,80]{1,0:T(8,128)} %get-tuple-element.65) | copy-start | bytes 184324
  241.2 7.6 %all-to-all-start.6 = ((f32[192,4,20]{0,2,1:T(8,128)}), f32[192,4,20]{0,2,1:T(8,128)S(1)}, u32[]{:S(2)}, u32[]{:S(2)}) async-start(f32[192,4,20]{0,2,1:T(8,128)} %all_to_all.38), calls=%async_computation.6 | async-start | bytes 196608 | tf_op jit(solution)/shard_map/all_to_all | solution.py:324
  (9 other events, 40.3 us)

commit v3 on v2

--- a/solution.py
+++ b/solution.py
@@ -1,5 +1,3 @@
-import functools
-
 import jax
 import jax.numpy as jnp
 from jax import lax
@@ -10,7 +8,7 @@
 F32, BF16, F16 = jnp.float32, jnp.bfloat16, jnp.float16
 TINY = 1e-30
 STEP_HEADS = 8
-STREAMS = 2
+STREAMS = 1
 
 
 def split(value):
@@ -46,12 +44,12 @@
 
 
 def within_kernel(
-    x_ref, dy_ref, cum_ref, cumt_ref, b_ref, c_ref, gain_ref, *rest, per, width, first,
+    x_ref, dy_ref, cum_ref, cumt_ref, b_ref, c_ref, gain_ref,
+    y_ref, dx_ref, dsc_ref, rows_ref, cols_ref, scores_ref, *, per, width,
 ):
-    y_ref, dx_ref, dsc_ref, rows_ref, cols_ref, scores_ref = rest[-6:]
-    step = pl.program_id(0) + first
-
-    @pl.when(step == first)
+    step = pl.program_id(0)
+
+    @pl.when(step == 0)
     def _():
         scores_ref[...] = dot(c_ref[...], b_ref[...], 1, 1)
         dsc_ref[...] = jnp.zeros_like(dsc_ref)
@@ -264,33 +262,19 @@
     sums_f, sums_b = own_state.reshape(shape), own_seed.reshape(shape)
     arrived = [swap(sums_f[:, at] * grow[0], sums_b[:, at] * grow[1]) for at in pieces]
 
-    def within(first, last, earlier):
-        wide_at = pl.BlockSpec((length, lane_block), lambda k: (0, k + first))
-        rows_at = pl.BlockSpec((per, length), lambda k: (k + first, 0))
-        gain_at = pl.BlockSpec((1, lane_block), lambda k: (0, k + first))
-        return pl.pallas_call(
-            functools.partial(within_kernel, per=per, width=width, first=first),
-            grid=(last - first,),
-            in_specs=[wide_at, wide_at, whole(length, heads), rows_at] + maps + [gain_at]
-            + [pl.BlockSpec(memory_space=pl.ANY)] * len(earlier),
-            out_specs=[wide_at, wide_at, whole(length, length), whole(length, heads), rows_at],
-            out_shape=[sd((length, channels), F32)] * 2
-            + [sd((length, length), F32), sd((length, heads), F32), sd((heads, length), F32)],
-            scratch_shapes=[pltpu.VMEM((length, length), F32)], name="within",
-            input_output_aliases=dict(zip((7, 8, 9), (0, 1, 4))) if earlier else {},
-            cost_estimate=pl.CostEstimate(
-                flops=24 * length * length * channels, transcendentals=0,
-                bytes_accessed=16 * length * channels,
-            ),
-        )(signal, cotangent, cum, cum_t, into, outof, gain_row, *earlier)
-
-    y_half, dx_half, dscores_a, rows_a, cols_half = within(0, steps // 2, ())
-    arrived[0], rows_a = lax.optimization_barrier((arrived[0], rows_a))
-
-    homes, ready = [], None
+    y_local, dx_local, dscores, rows, cols = call(
+        within_kernel, "within",
+        [wide, wide, whole(length, heads), pl.BlockSpec((per, length), lambda k: (k, 0))] + maps
+        + [pl.BlockSpec((1, lane_block), lambda k: (0, k))],
+        [wide, wide, whole(length, length), whole(length, heads),
+         pl.BlockSpec((per, length), lambda k: (k, 0))],
+        [sd((length, channels), F32)] * 2
+        + [sd((length, length), F32), sd((length, heads), F32), sd((heads, length), F32)],
+        scratch=[pltpu.VMEM((length, length), F32)], flops=24 * length * length * channels,
+    )(signal, cotangent, cum, cum_t, into, outof, gain_row)
+
+    homes = []
     for at, (parts_f, parts_b) in zip(pieces, arrived):
-        if ready is not None:
-            parts_f, parts_b, ready = lax.optimization_barrier((parts_f, parts_b, ready))
         parts_f, parts_b = parts_f.astype(F32), parts_b.astype(F32)
         keep = jnp.exp(logs[:, at])[:, :, None, None]
         group_f, group_b = parts_f[0], parts_b[-1]
@@ -299,13 +283,10 @@
             group_b = keep[members - 1 - s] * group_b + parts_b[members - 1 - s]
         list_f = [chain(group_f, block_logs[:, at], "ctx", False)]
         list_b = [chain(group_b, block_logs[:, at], "ctx", True)]
-        ready = list_f[0][0, :8] + list_b[0][0, :8]
         for s in range(members - 1):
             list_f.append(keep[s] * list_f[-1] + parts_f[s])
             list_b.append(keep[members - 1 - s] * list_b[-1] + parts_b[members - 1 - s])
         homes.append(swap(jnp.stack(list_f), jnp.stack(list_b[::-1])))
-    y_local, dx_local, dscores_b, rows_b, cols = within(steps // 2, steps, (y_half, dx_half, cols_half))
-    dscores, rows = dscores_a + dscores_b, rows_a + rows_b
     e_all = jnp.concatenate([h[0] for h in homes], axis=1).astype(F32) / grow[0]
     l_all = jnp.concatenate([h[1] for h in homes], axis=1).astype(F32) / grow[1]
     e_all, l_all = e_all.reshape(channels, state), l_all.reshape(channels, state)

time: 251 us -> 232 us (0.924)
  the two profiles are of different devices: /device:TPU:0 before, /device:TPU:25 now
where the time goes in v3:
time: 232 us; the launch traced here: 231 us
  waiting for transfers between devices  87.9 us (38%)
  Pallas kernels  55.2 us (24%)
  starting transfers between devices  40 us (17%)
  other arithmetic  26.2 us (11%)
  local copies, waits for them, and re-layouts  11.3 us (5%)
  blocking collectives  8.97 us (4%)
    ppermute x6, waiting for transfers between devices, chain(): got = lax.ppermute(own.astype(F16), axis, pairs).astype(F32)  56.6 us
    all_to_all x2, waiting for transfers between devices, swap(): both = lax.all_to_all(both, 'head', split_axis=0, concat_axis=0, tiled=True)  30 us
    pallas_call x1, Pallas kernels, shards(): call(within_kernel, 'within', [wide, wide, whole(length, heads), pl.Block...  27.9 us
    ppermute x6, starting transfers between devices, chain(): got = lax.ppermute(own.astype(F16), axis, pairs).astype(F32)  16 us
    pallas_call x1, Pallas kernels, shards(): call(carried_kernel, 'carried', [wide, wide, wide, wide, tall, tall, whol...  15.5 us
    pallas_call x1, Pallas kernels, shards(): call(states_kernel, 'states', [wide, wide, whole(length, heads)] + maps,...  11.8 us
    all_to_all x2, starting transfers between devices, swap(): both = lax.all_to_all(both, 'head', split_axis=0, concat_axis=0, tiled=True)  11.1 us
    all_gather x1, blocking collectives, shards(): lax.all_gather(jnp.concatenate([grad_in, grad_out], axis=1), 'head', tile...  8.97 us
  transfers between devices with their start and end apart: 11, of which 8 were waited for; matrix products, arithmetic and copies ran while one was open for 4% of the time, Pallas kernels for 17%

profile of v3, /device:TPU:25, one launch (start us, length us, event | category | flops | bytes accessed | tf_op | source)
XLA Modules:
  0.0 230.8 jit_solution(13137288572076907505)
XLA Ops:
  0.7 2.6 %abs_reduce_fusion = bf16[]{:T(256)} fusion(bf16[192,5120]{1,0:T(8,128)(2,1)} %refs_1_.5), kind=kLoop, calls=%fused_computation.6 | loop fusion | flops 1966079 | bytes 1966082 | tf_op jit(solution)/shard_map/reduce_max | solution.py:185
  6.6 3.9 %all-to-all-start = ((f32[4,200,20]{1,2,0:T(8,128)}), f32[4,200,20]{1,2,0:T(8,128)S(1)}, u32[]{:S(2)}, u32[]{:S(2)}) async-start(f32[4,200,20]{1,2,0:T(8,128)} %copy.43), calls=%async_computation | async-start | bytes 196608 | tf_op jit(solution)/shard_map/all_to_all | solution.py:203
  18.1 5.5 %all-to-all-start.1 = ((f32[8,3,20]{2,1,0:T(4,128)}), f32[8,3,20]{2,1,0:T(4,128)S(1)}, u32[]{:S(2)}, u32[]{:S(2)}) async-start(f32[8,3,20]{2,1,0:T(4,128)} %broadcast_in_dim.14), calls=%async_computation.1 | async-start | bytes 32768 | tf_op jit(solution)/shard_map/all_to_all | solution.py:211
  24.5 11.8 %states.1 = (f32[5120,128]{1,0:T(8,128)}, f32[5120,128]{1,0:T(8,128)}) custom-call(bf16[192,5120]{1,0:T(8,128)(2,1)} %refs_0_.5, bf16[192,5120]{1,0:T(8,128)(2,1)} %refs_1_.5, f32[192,80]{1,0:T(8,128)} %copy.44.refs_2_.refs_6_, bf16[192,128]{1,0:T(8,128)(2,1)} %get-tuple-element.91.refs_4_.refs_3_.refs_7_, ...), custom_call_target="tpu_custom_call" | custom-call | flops 1006632960 | bytes 15728640 | tf_op jit(solution)/shard_map/states/pallas_call | solution.py:246
  37.1 2.6 %multiply_convert_fusion.1 = f16[5120,128]{1,0:T(8,128)(2,1)S(1)} fusion(f32[5120,128]{1,0:T(8,128)} %get-tuple-element.43, f32[]{:T(128)} %bitcast.11), kind=kLoop, calls=%fused_computation.5 | loop fusion | flops 1310720 | bytes 3932164 | tf_op jit(solution)/shard_map/convert_element_type | solution.py:256
  40.6 2.3 pad_maximum_fusion
  42.9 5.1 %all-to-all-start.2 = ((f16[4,1280,256]{2,1,0:T(8,128)(2,1)}), f16[4,1280,256]{2,1,0:T(8,128)(2,1)S(1)}, u32[]{:S(2)}, u32[]{:S(2)}) async-start(f16[4,1280,256]{2,1,0:T(8,128)(2,1)} %pad_maximum_fusion), calls=%async_computation.2 | async-start | bytes 5242880 | tf_op jit(solution)/shard_map/all_to_all | solution.py:258
  48.3 30.0 %all-to-all-done.2 = f16[4,1280,256]{2,1,0:T(8,128)(2,1)S(1)} async-done(((f16[4,1280,256]{2,1,0:T(8,128)(2,1)}), f16[4,1280,256]{2,1,0:T(8,128)(2,1)S(1)}, u32[]{:S(2)}, u32[]{:S(2)}) %all-to-all-start.2) | async-done | bytes 2621472 | tf_op jit(solution)/shard_map/all_to_all | solution.py:258
  79.6 3.1 %collective-permute-start.3 = (f16[20,64,128]{2,1,0:T(8,128)(2,1)S(1)}, f16[20,64,128]{2,1,0:T(8,128)(2,1)S(1)}, u32[]{:S(2)}, u32[]{:S(2)}) collective-permute-start(f16[20,64,128]{2,1,0:T(8,128)(2,1)S(1)} %get-tuple-element.63), channel_id=1, source_target_pairs={{4,0},{8,4},{12,8},{16,12},{20,16},{24,20},{28,24},{5,1},{9,5},{13... | collective-permute-start | bytes 983048 | tf_op jit(solution)/shard_map/ppermute | solution.py:165
  82.7 7.0 %collective-permute-done.3 = f16[20,64,128]{2,1,0:T(8,128)(2,1)S(1)} collective-permute-done((f16[20,64,128]{2,1,0:T(8,128)(2,1)S(1)}, f16[20,64,128]{2,1,0:T(8,128)(2,1)S(1)}, u32[]{:S(2)}, u32[]{:S(2)}) %collective-permute-start.3) | collective-permute-done | bytes 327712 | tf_op jit(solution)/shard_map/ppermute | solution.py:165
  90.0 2.2 collective-permute-start.4
  92.2 5.2 %collective-permute-done.4 = f16[20,64,128]{2,1,0:T(8,128)(2,1)S(1)} collective-permute-done((f16[20,64,128]{2,1,0:T(8,128)(2,1)S(1)}, f16[20,64,128]{2,1,0:T(8,128)(2,1)S(1)}, u32[]{:S(2)}, u32[]{:S(2)}) %collective-permute-start.4) | collective-permute-done | bytes 327712 | tf_op jit(solution)/shard_map/ppermute | solution.py:165
  97.6 4.1 %collective-permute-start.5 = (f16[20,64,128]{2,1,0:T(8,128)(2,1)S(1)}, f16[20,64,128]{2,1,0:T(8,128)(2,1)S(1)}, u32[]{:S(2)}, u32[]{:S(2)}) collective-permute-start(f16[20,64,128]{2,1,0:T(8,128)(2,1)S(1)} %fusion.7), channel_id=1, source_target_pairs={{16,0},{20,4},{24,8},{28,12},{17,1},{21,5},{25,9},{29,13},{18,2},{... | collective-permute-start | bytes 983048 | tf_op jit(solution)/shard_map/ppermute | solution.py:165
  101.8 4.4 %collective-permute-done.5 = f16[20,64,128]{2,1,0:T(8,128)(2,1)S(1)} collective-permute-done((f16[20,64,128]{2,1,0:T(8,128)(2,1)S(1)}, f16[20,64,128]{2,1,0:T(8,128)(2,1)S(1)}, u32[]{:S(2)}, u32[]{:S(2)}) %collective-permute-start.5) | collective-permute-done | bytes 327712 | tf_op jit(solution)/shard_map/ppermute | solution.py:165
  106.8 4.0 %collective-permute-start = (f16[20,64,128]{2,1,0:T(8,128)(2,1)S(1)}, f16[20,64,128]{2,1,0:T(8,128)(2,1)S(1)}, u32[]{:S(2)}, u32[]{:S(2)}) collective-permute-start(f16[20,64,128]{2,1,0:T(8,128)(2,1)S(1)} %get-tuple-element.59), channel_id=1, source_target_pairs={{0,4},{4,8},{8,12},{12,16},{16,20},{20,24},{24,28},{1,5},{5,9},{9,... | collective-permute-start | bytes 983048 | tf_op jit(solution)/shard_map/ppermute | solution.py:165
  110.8 15.7 %collective-permute-done = f16[20,64,128]{2,1,0:T(8,128)(2,1)S(1)} collective-permute-done((f16[20,64,128]{2,1,0:T(8,128)(2,1)S(1)}, f16[20,64,128]{2,1,0:T(8,128)(2,1)S(1)}, u32[]{:S(2)}, u32[]{:S(2)}) %collective-permute-start) | collective-permute-done | bytes 327712 | tf_op jit(solution)/shard_map/ppermute | solution.py:165
  128.0 7.9 %collective-permute-done.1 = f16[20,64,128]{2,1,0:T(8,128)(2,1)S(1)} collective-permute-done((f16[20,64,128]{2,1,0:T(8,128)(2,1)S(1)}, f16[20,64,128]{2,1,0:T(8,128)(2,1)S(1)}, u32[]{:S(2)}, u32[]{:S(2)}) %collective-permute-start.1) | collective-permute-done | bytes 327712 | tf_op jit(solution)/shard_map/ppermute | solution.py:165
  137.5 16.4 %collective-permute-done.2 = f16[20,64,128]{2,1,0:T(8,128)(2,1)S(1)} collective-permute-done((f16[20,64,128]{2,1,0:T(8,128)(2,1)S(1)}, f16[20,64,128]{2,1,0:T(8,128)(2,1)S(1)}, u32[]{:S(2)}, u32[]{:S(2)}) %collective-permute-start.2) | collective-permute-done | bytes 327712 | tf_op jit(solution)/shard_map/ppermute | solution.py:165
  156.9 5.9 %all-to-all-start.3 = ((f16[4,1280,256]{2,1,0:T(8,128)(2,1)}), f16[4,1280,256]{2,1,0:T(8,128)(2,1)S(1)}, u32[]{:S(2)}, u32[]{:S(2)}) async-start(f16[4,1280,256]{2,1,0:T(8,128)(2,1)} %maximum_maximum_fusion), calls=%async_computation.3 | async-start | bytes 5242880 | tf_op jit(solution)/shard_map/all_to_all | solution.py:258
  163.9 27.9 %within.1 = (f32[192,5120]{1,0:T(8,128)}, f32[192,5120]{1,0:T(8,128)}, f32[192,192]{1,0:T(8,128)}, f32[192,80]{1,0:T(8,128)}, f32[80,192]{1,0:T(8,128)}) custom-call(bf16[192,5120]{1,0:T(8,128)(2,1)} %refs_0_.5, bf16[192,5120]{1,0:T(8,128)(2,1)} %refs_1_.5, f32[192,80]{1,0:T(8,128)} %copy.44.refs_2_.refs_6_, f32[80,192]{1,0:T(8,128)} %bitcast.148, ...), custom_call_target="tpu_custom_call" | custom-call | flops 4529848320 | bytes 15728640 | tf_op jit(solution)/shard_map/within/pallas_call | solution.py:265
  194.3 4.2 %convert_divide_fusion = (f32[4,20,64,128]{3,2,1,0:T(8,128)}, f32[4,20,64,128]{3,2,1,0:T(8,128)}) fusion(f16[4,20,64,256]{3,2,1,0:T(8,128)(2,1)S(1)} %bitcast.131, f32[]{:T(128)} %bitcast.13, f32[]{:T(128)} %bitcast.11), kind=kLoop, calls=%fused_computation.2 | loop fusion | flops 2621440 | bytes 7864328 | tf_op jit(solution)/shard_map/div | solution.py:291
  198.5 15.5 %carried.1 = (bf16[192,5120]{1,0:T(8,128)(2,1)}, bf16[192,5120]{1,0:T(8,128)(2,1)}, f32[192,128]{1,0:T(8,128)}, f32[192,128]{1,0:T(8,128)}, f32[192,80]{1,0:T(8,128)}) custom-call(bf16[192,5120]{1,0:T(8,128)(2,1)} %refs_0_.5, bf16[192,5120]{1,0:T(8,128)(2,1)} %refs_1_.5, f32[192,5120]{1,0:T(8,128)} %get-tuple-element.41.refs_2_, ...), custom_call_target="tpu_custom_call" | custom-call | flops 2516582400 | bytes 15728640 | tf_op jit(solution)/shard_map/carried/pallas_call | solution.py:294
  215.7 3.5 %all-to-all-start.4 = ((f32[192,4,20]{0,2,1:T(8,128)}), f32[192,4,20]{0,2,1:T(8,128)S(1)}, u32[]{:S(2)}, u32[]{:S(2)}) async-start(f32[192,4,20]{0,2,1:T(8,128)} %all_to_all.30), calls=%async_computation.4 | async-start | bytes 196608 | tf_op jit(solution)/shard_map/all_to_all | solution.py:305
  220.1 9.0 %all_gather.3 = f32[768,256]{1,0:T(8,128)S(1)} all-gather(f32[192,256]{1,0:T(8,128)S(1)} %pad_maximum_fusion.1), channel_id=1, replica_groups=mesh['ctx'=8,'head'=4] {'head'}, dimensions={0}, use_global_device_ids=true | all-gather | bytes 983040 | tf_op jit(solution)/shard_map/all_gather | solution.py:304
  (87 shorter events, 30.1 us)
Async XLA Ops:
  0.6 2.6 %copy-start = (bf16[192,5120]{1,0:T(8,128)(2,1)S(1)}, bf16[192,5120]{1,0:T(8,128)(2,1)}, u32[]{:S(2)}) copy-start(bf16[192,5120]{1,0:T(8,128)(2,1)} %refs_0_.5) | copy-start | bytes 5898244
  0.6 4.8 %copy-start.6 = (f32[20]{0:T(128)S(1)}, f32[20]{0:T(128)}, u32[]{:S(2)}) copy-start(f32[20]{0:T(128)} %param.15) | copy-start | bytes 244
  0.7 5.1 %copy-start.5 = (f32[768,20]{0,1:T(8,128)S(1)}, f32[768,20]{0,1:T(8,128)}, u32[]{:S(2)}) copy-start(f32[768,20]{0,1:T(8,128)} %param.14) | copy-start | bytes 184324
  0.7 9.9 %copy-start.3 = (bf16[768,128]{1,0:T(8,128)(2,1)S(1)}, bf16[768,128]{1,0:T(8,128)(2,1)}, u32[]{:S(2)}) copy-start(bf16[768,128]{1,0:T(8,128)(2,1)} %param.13) | copy-start | bytes 589828
  0.7 10.5 %copy-start.4 = (bf16[768,128]{1,0:T(8,128)(2,1)S(1)}, bf16[768,128]{1,0:T(8,128)(2,1)}, u32[]{:S(2)}) copy-start(bf16[768,128]{1,0:T(8,128)(2,1)} %param.12) | copy-start | bytes 589828
  6.6 7.3 %all-to-all-start = ((f32[4,200,20]{1,2,0:T(8,128)}), f32[4,200,20]{1,2,0:T(8,128)S(1)}, u32[]{:S(2)}, u32[]{:S(2)}) async-start(f32[4,200,20]{1,2,0:T(8,128)} %copy.43), calls=%async_computation | async-start | bytes 196608 | tf_op jit(solution)/shard_map/all_to_all | solution.py:203
  18.1 18.3 %all-to-all-start.1 = ((f32[8,3,20]{2,1,0:T(4,128)}), f32[8,3,20]{2,1,0:T(4,128)S(1)}, u32[]{:S(2)}, u32[]{:S(2)}) async-start(f32[8,3,20]{2,1,0:T(4,128)} %broadcast_in_dim.14), calls=%async_computation.1 | async-start | bytes 32768 | tf_op jit(solution)/shard_map/all_to_all | solution.py:211
  23.8 15.9 %copy-start.2 = (f32[192,80]{0,1:T(8,128)}, f32[192,80]{0,1:T(8,128)S(1)}, u32[]{:S(2)}) copy-start(f32[192,80]{0,1:T(8,128)S(1)} %fusion.14) | copy-start | bytes 184324
  36.3 3.4 %copy-start.1 = (f32[5120,128]{1,0:T(8,128)S(1)}, f32[5120,128]{1,0:T(8,128)}, u32[]{:S(2)}) copy-start(f32[5120,128]{1,0:T(8,128)} %get-tuple-element.44) | copy-start | bytes 7864324
  42.9 35.5 %all-to-all-start.2 = ((f16[4,1280,256]{2,1,0:T(8,128)(2,1)}), f16[4,1280,256]{2,1,0:T(8,128)(2,1)S(1)}, u32[]{:S(2)}, u32[]{:S(2)}) async-start(f16[4,1280,256]{2,1,0:T(8,128)(2,1)} %pad_maximum_fusion), calls=%async_computation.2 | async-start | bytes 5242880 | tf_op jit(solution)/shard_map/all_to_all | solution.py:258
  79.6 10.2 %collective-permute-start.3 = (f16[20,64,128]{2,1,0:T(8,128)(2,1)S(1)}, f16[20,64,128]{2,1,0:T(8,128)(2,1)S(1)}, u32[]{:S(2)}, u32[]{:S(2)}) collective-permute-start(f16[20,64,128]{2,1,0:T(8,128)(2,1)S(1)} %get-tuple-element.63), channel_id=1, source_target_pairs={{4,0},{8,4},{12,8},{16,12},{20,16},{24,20},{28,24},{5,1},{9,5},{13... | collective-permute-start | bytes 983048 | tf_op jit(solution)/shard_map/ppermute | solution.py:165
  90.0 7.4 %collective-permute-start.4 = (f16[20,64,128]{2,1,0:T(8,128)(2,1)S(1)}, f16[20,64,128]{2,1,0:T(8,128)(2,1)S(1)}, u32[]{:S(2)}, u32[]{:S(2)}) collective-permute-start(f16[20,64,128]{2,1,0:T(8,128)(2,1)S(1)} %fusion.10), channel_id=1, source_target_pairs={{8,0},{12,4},{16,8},{20,12},{24,16},{28,20},{9,1},{13,5},{17,9},{2... | collective-permute-start | bytes 983048 | tf_op jit(solution)/shard_map/ppermute | solution.py:165
  97.6 8.6 %collective-permute-start.5 = (f16[20,64,128]{2,1,0:T(8,128)(2,1)S(1)}, f16[20,64,128]{2,1,0:T(8,128)(2,1)S(1)}, u32[]{:S(2)}, u32[]{:S(2)}) collective-permute-start(f16[20,64,128]{2,1,0:T(8,128)(2,1)S(1)} %fusion.7), channel_id=1, source_target_pairs={{16,0},{20,4},{24,8},{28,12},{17,1},{21,5},{25,9},{29,13},{18,2},{... | collective-permute-start | bytes 983048 | tf_op jit(solution)/shard_map/ppermute | solution.py:165
  106.8 19.7 %collective-permute-start = (f16[20,64,128]{2,1,0:T(8,128)(2,1)S(1)}, f16[20,64,128]{2,1,0:T(8,128)(2,1)S(1)}, u32[]{:S(2)}, u32[]{:S(2)}) collective-permute-start(f16[20,64,128]{2,1,0:T(8,128)(2,1)S(1)} %get-tuple-element.59), channel_id=1, source_target_pairs={{0,4},{4,8},{8,12},{12,16},{16,20},{20,24},{24,28},{1,5},{5,9},{9,... | collective-permute-start | bytes 983048 | tf_op jit(solution)/shard_map/ppermute | solution.py:165
  126.7 9.2 %collective-permute-start.1 = (f16[20,64,128]{2,1,0:T(8,128)(2,1)S(1)}, f16[20,64,128]{2,1,0:T(8,128)(2,1)S(1)}, u32[]{:S(2)}, u32[]{:S(2)}) collective-permute-start(f16[20,64,128]{2,1,0:T(8,128)(2,1)S(1)} %fusion.11), channel_id=1, source_target_pairs={{0,8},{4,12},{8,16},{12,20},{16,24},{20,28},{1,9},{5,13},{9,17},{1... | collective-permute-start | bytes 983048 | tf_op jit(solution)/shard_map/ppermute | solution.py:165
  136.2 17.8 %collective-permute-start.2 = (f16[20,64,128]{2,1,0:T(8,128)(2,1)S(1)}, f16[20,64,128]{2,1,0:T(8,128)(2,1)S(1)}, u32[]{:S(2)}, u32[]{:S(2)}) collective-permute-start(f16[20,64,128]{2,1,0:T(8,128)(2,1)S(1)} %fusion.3), channel_id=1, source_target_pairs={{0,16},{4,20},{8,24},{12,28},{1,17},{5,21},{9,25},{13,29},{2,18},{... | collective-permute-start | bytes 983048 | tf_op jit(solution)/shard_map/ppermute | solution.py:165
  156.9 37.4 %all-to-all-start.3 = ((f16[4,1280,256]{2,1,0:T(8,128)(2,1)}), f16[4,1280,256]{2,1,0:T(8,128)(2,1)S(1)}, u32[]{:S(2)}, u32[]{:S(2)}) async-start(f16[4,1280,256]{2,1,0:T(8,128)(2,1)} %maximum_maximum_fusion), calls=%async_computation.3 | async-start | bytes 5242880 | tf_op jit(solution)/shard_map/all_to_all | solution.py:258
  215.7 14.4 %all-to-all-start.4 = ((f32[192,4,20]{0,2,1:T(8,128)}), f32[192,4,20]{0,2,1:T(8,128)S(1)}, u32[]{:S(2)}, u32[]{:S(2)}) async-start(f32[192,4,20]{0,2,1:T(8,128)} %all_to_all.30), calls=%async_computation.4 | async-start | bytes 196608 | tf_op jit(solution)/shard_map/all_to_all | solution.py:305
